TPU v7x, 32 devices: a whole 2x2x4 slice. The times are simulated.
32 devices in a mesh: row: 4 (over y, core), col: 8 (over z, x).
Axes of the slice: x: 2, y: 2, z: 4, core: 2. Of those that a mesh axis runs over, the one named last changes fastest.
Arguments:
- transfer: bfloat16 [2048, 2, 512, 256], P(('row', 'col')), may hold values from -0.65625 to 0.65625
- target: bfloat16 [2048, 2, 32, 512], P(('row', 'col')), may hold values from -6 to 6
- zone_mask: int32 [32, 512], replicated, may hold values 0 or 1
- dark_weight: float32 [32], replicated, may hold values from 1 to 4
- reg_weight: float32 [2048], P(('row', 'col')), may hold values from 0.05 to 2
- momentum: float32 [1], replicated, may hold values from 0.2 to 0.8
Outputs:
- filters: float32 [32, 256, 1024], P(None, ('row', 'col'))
- residual: float32 [32, 256, 1024], P(None, ('row', 'col'))
All inputs are finite; a program needn't handle non-finite values.
Results may differ from a plain program's by a relative error of at most 0.0059.
Values may be sent and summed in bfloat16 or wider, within the bound.
No kernel may reach another device: no remote copies, remote signals or barrier semaphores. Data moves between devices by JAX's collectives and lax.ppermute only.
A program may use at most 128 MiB of HBM per device.

v0:
```python
import math

import jax
import jax.numpy as jnp
from jax import lax
from jax.sharding import PartitionSpec as P

K = 1024
F = 2048
ITERS = 2


def build_table(taps, bins):
    tap_index = jnp.arange(taps, dtype=jnp.int32)[:, None]
    bin_index = jnp.arange(bins, dtype=jnp.int32)[None, :]
    phase = (tap_index * bin_index % bins).astype(jnp.float32) * (2.0 * math.pi / bins)
    return jnp.stack([jnp.cos(phase), -jnp.sin(phase)], axis=1) / math.sqrt(bins)


def body(transfer, target, zone_mask, dark_weight, reg_weight, momentum):
    dft_table = build_table(K, F)
    mic_gains = jnp.where(zone_mask == 1, jnp.float32(1.0), dark_weight[:, None])
    weight_real = transfer[:, 0]
    weight_imag = transfer[:, 1]
    reg_term = reg_weight[:, None, None]

    def to_taps(spectrum):
        regrouped = lax.all_to_all(
            spectrum, ("row", "col"), split_axis=3, concat_axis=0, tiled=True
        )
        return jnp.einsum("fctl,kcf->tlk", regrouped, dft_table, precision=lax.Precision.HIGHEST)

    def back_project(err_real, err_imag):
        back_real = jnp.einsum(
            "fml,ftm->ftl", weight_real, err_real, preferred_element_type=jnp.float32
        )
        back_real = back_real + jnp.einsum(
            "fml,ftm->ftl", weight_imag, err_imag, preferred_element_type=jnp.float32
        )
        back_imag = jnp.einsum(
            "fml,ftm->ftl", weight_real, err_imag, preferred_element_type=jnp.float32
        )
        back_imag = back_imag - jnp.einsum(
            "fml,ftm->ftl", weight_imag, err_real, preferred_element_type=jnp.float32
        )
        return (back_real, back_imag)

    rhs_error = jnp.where(zone_mask[None, None] == 1, target, jnp.zeros_like(target))
    rhs_real, rhs_imag = back_project(rhs_error[:, 0], rhs_error[:, 1])
    rhs = to_taps(jnp.stack([rhs_real, rhs_imag], axis=1))
    filters = jnp.zeros_like(rhs)
    residual = rhs
    direction = rhs
    for iteration in range(ITERS):
        along_term = jnp.sum(residual * direction)
        to_spectrum = jnp.einsum(
            "tlk,kcf->fctl", direction, dft_table, precision=lax.Precision.HIGHEST
        ).astype(jnp.bfloat16)
        to_regrouped = lax.all_to_all(
            to_spectrum, ("row", "col"), split_axis=0, concat_axis=3, tiled=True
        )
        spec_real = to_regrouped[:, 0]
        spec_imag = to_regrouped[:, 1]
        press_real = jnp.einsum(
            "fml,ftl->ftm", weight_real, spec_real, preferred_element_type=jnp.float32
        )
        press_real = press_real - jnp.einsum(
            "fml,ftl->ftm", weight_imag, spec_imag, preferred_element_type=jnp.float32
        )
        press_imag = jnp.einsum(
            "fml,ftl->ftm", weight_real, spec_imag, preferred_element_type=jnp.float32
        )
        press_imag = press_imag + jnp.einsum(
            "fml,ftl->ftm", weight_imag, spec_real, preferred_element_type=jnp.float32
        )
        weighted_real = mic_gains * press_real
        weighted_imag = mic_gains * press_imag
        operator_back_real, operator_back_imag = back_project(
            weighted_real.astype(jnp.bfloat16), weighted_imag.astype(jnp.bfloat16)
        )
        wide_real = spec_real.astype(jnp.float32)
        wide_imag = spec_imag.astype(jnp.float32)
        totals = None
        combined = jnp.stack(
            [operator_back_real + reg_term * wide_real, operator_back_imag + reg_term * wide_imag],
            axis=1,
        )
        image_taps, totals = (to_taps(combined), totals)
        along_sum, bend_sum = lax.psum(
            (along_term, jnp.sum(direction * image_taps)), ("row", "col")
        )
        step_size = along_sum / bend_sum
        filters = filters + step_size * direction
        residual = residual - step_size * image_taps
        if iteration + 1 < ITERS:
            direction = residual + momentum[iteration] * direction
    return (filters, residual)


def solution(mesh):
    in_specs = (
        P(("row", "col"), None, None, None),
        P(("row", "col"), None, None, None),
        P(),
        P(),
        P(("row", "col")),
        P(),
    )
    out_specs = (P(None, ("row", "col"), None), P(None, ("row", "col"), None))
    return jax.shard_map(body, mesh=mesh, in_specs=in_specs, out_specs=out_specs, check_vma=False)
```

profile of v0, /device:TPU:0, one launch (start us, length us, event | category | flops | bytes accessed | tf_op | source)
XLA Modules:
  0.0 1125.3 jit_solution(2938262932582563198)
XLA Ops:
  61.9 34.6 %sine_negate_fusion = (f32[1024,1,2048]{2,0,1:T(8,128)}, f32[1024,1,2048]{2,0,1:T(8,128)}) fusion(), kind=kLoop, calls=%fused_computation.57 | loop fusion | flops 31457280 | bytes 16777216 | tf_op jit(solution)/shard_map/neg | solution.py:17
  96.5 60.6 %all-to-all-done = f32[32,1,32768]{2,1,0:T(1,128)} async-done(((f32[32,1,32768]{2,1,0:T(1,128)}), f32[32,1,32768]{2,1,0:T(1,128)}, u32[]{:S(2)}, u32[]{:S(2)}) %all-to-all-start) | async-done | bytes 4194336 | tf_op jit(solution)/shard_map/all_to_all | solution.py:28
  157.7 13.8 %reduce = f32[32,32768]{1,0:T(8,128)} reduce(f32[32,1,32768]{2,1,0:T(1,128)} %all-to-all-done, f32[]{:T(128)} %broadcast.90), dimensions={1}, to_apply=%all_to_all.65.reduce_sub_computation | reduce | bytes 8388612 | tf_op jit(solution)/shard_map/all_to_all | solution.py:28
  198.1 18.8 %fusion.81 = f32[32,8,1024]{2,1,0:T(8,128)S(1)} fusion(f32[2048,2,32,8]{0,3,1,2:T(8,128)} %all_to_all.68, f32[1024,1,2048]{2,0,1:T(8,128)} %get-tuple-element.20, f32[1024,1,2048]{2,0,1:T(8,128)} %get-tuple-element.21), kind=kOutput, calls=%fused_computation.90 | convolution fusion | flops 12893290496 | bytes 22020096 | tf_op jit(solution)/shard_map/fctl,kcf->tlk/dot_general | solution.py:31
  217.8 19.9 %fusion.66 = bf16[2048,2,32,8]{0,2,3,1:T(8,128)(2,1)S(1)} fusion(f32[32,8,1024]{2,1,0:T(8,128)S(1)} %fusion.81, f32[1024,1,2048]{2,0,1:T(8,128)} %get-tuple-element.20, f32[1024,1,2048]{2,0,1:T(8,128)} %get-tuple-element.21), kind=kOutput, calls=%fused_computation.73 | convolution fusion | flops 12894339072 | bytes 19922944 | tf_op jit(solution)/shard_map/tlk,kcf->fctl/dot_general | solution.py:56
  246.3 12.2 %reshape.86 = bf16[32,2,16384]{2,1,0:T(2,128)(2,1)S(1)} reshape(bf16[2048,2,8,32]{3,2,1,0:T(8,128)(2,1)} %bitcast.200) | data formatting | bytes 4194304
  258.6 52.9 %all_to_all.90 = bf16[32,2,16384]{2,1,0:T(2,128)(2,1)} all-to-all(bf16[32,2,16384]{2,1,0:T(2,128)(2,1)S(1)} %reshape.86), channel_id=1, replica_groups=mesh['row'=4,'col'=8] {'row','col'}, dimensions={0} | all-to-all | bytes 4194304 | tf_op jit(solution)/shard_map/all_to_all | solution.py:59
  323.2 12.1 %copy.65 = bf16[32,64,2,32,8]{1,4,0,3,2:T(8,128)(2,1)} copy(bf16[32,64,2,32,8]{3,4,2,1,0:T(8,128)(2,1)} %bitcast.201) | data formatting | bytes 4194304 | tf_op jit(solution)/shard_map/all_to_all | solution.py:59
  342.7 12.7 %fusion.12 = f32[64,32,512]{2,1,0:T(8,128)} fusion(bf16[64,1,32,256]{3,2,0,1:T(8,128)(2,1)S(1)} %copy.88, bf16[64,2,512,256]{3,2,1,0:T(8,128)(2,1)} %param.6), kind=kOutput, calls=%fused_computation.13 | convolution fusion | flops 536870912 | bytes 22020096 | tf_op jit(solution)/shard_map/fml,ftl->ftm/dot_general | solution.py:73
  355.4 12.7 %fusion.34 = f32[64,32,512]{2,1,0:T(8,128)} fusion(bf16[64,1,32,256]{3,2,0,1:T(8,128)(2,1)S(1)} %copy.88, bf16[64,2,512,256]{3,2,1,0:T(8,128)(2,1)} %param.6), kind=kOutput, calls=%fused_computation.35 | convolution fusion | flops 536870912 | bytes 22020096 | tf_op jit(solution)/shard_map/fml,ftl->ftm/dot_general | solution.py:64
  371.0 12.7 %fusion.30 = f32[64,32,512]{2,1,0:T(8,128)} fusion(bf16[64,1,32,256]{3,2,0,1:T(8,128)(2,1)S(1)} %copy.89, bf16[64,2,512,256]{3,2,1,0:T(8,128)(2,1)} %param.6), kind=kOutput, calls=%fused_computation.31 | convolution fusion | flops 536870912 | bytes 22020096 | tf_op jit(solution)/shard_map/fml,ftl->ftm/dot_general | solution.py:70
  383.7 12.7 %fusion.14 = f32[64,32,512]{2,1,0:T(8,128)} fusion(bf16[64,1,32,256]{3,2,0,1:T(8,128)(2,1)S(1)} %copy.89, bf16[64,2,512,256]{3,2,1,0:T(8,128)(2,1)} %param.6), kind=kOutput, calls=%fused_computation.15 | convolution fusion | flops 536870912 | bytes 22020096 | tf_op jit(solution)/shard_map/fml,ftl->ftm/dot_general | solution.py:67
  420.2 12.8 %add_bitcast_fusion.3 = f32[64,1,32,256]{3,2,0,1:T(8,128)} fusion(f32[64,32,256]{2,1,0:T(8,128)} %fusion.10, f32[64,32,512]{2,1,0:T(8,128)} %fusion.34, f32[64,32,512]{2,1,0:T(8,128)} %fusion.14, f32[32,512]{1,0:T(8,128)S(1)} %get-tuple-element.10, bf16[64,1,32,256]{3,2,0,1:T(8,128)(2,1)S(1)} %copy.88, f32[64]{0:T(128)S(1)} %copy-done.9, ...), kind=kOutput, calls=%fused_computation.79 | convolution fusion | flops 542113792 | bytes 30474496 | tf_op jit(solution)/shard_map/fml,ftm->ftl/dot_general | solution.py:34
  433.1 13.3 %add_bitcast_fusion.2 = f32[64,1,32,256]{3,2,0,1:T(8,128)} fusion(f32[64,32,256]{2,1,0:T(8,128)} %fusion.8, f32[64,32,512]{2,1,0:T(8,128)} %fusion.30, f32[64,32,512]{2,1,0:T(8,128)} %fusion.12, f32[32,512]{1,0:T(8,128)S(1)} %get-tuple-element.10, bf16[64,1,32,256]{3,2,0,1:T(8,128)(2,1)S(1)} %copy.89, f32[64]{0:T(128)S(1)} %copy-done.9, ...), kind=kOutput, calls=%fused_computation.78 | convolution fusion | flops 542113792 | bytes 30474496 | tf_op jit(solution)/shard_map/fml,ftm->ftl/dot_general | solution.py:40
  473.6 94.5 %all-to-all-done.2 = f32[32,1,32768]{2,1,0:T(1,128)} async-done(((f32[32,1,32768]{2,1,0:T(1,128)}), f32[32,1,32768]{2,1,0:T(1,128)}, u32[]{:S(2)}, u32[]{:S(2)}) %all-to-all-start.2) | async-done | bytes 4194336 | tf_op jit(solution)/shard_map/all_to_all | solution.py:28
  568.1 13.8 %reduce.1 = f32[32,32768]{1,0:T(8,128)} reduce(f32[32,1,32768]{2,1,0:T(1,128)} %all-to-all-done.2, f32[]{:T(128)} %broadcast.90), dimensions={1}, to_apply=%all_to_all.73.reduce_sub_computation | reduce | bytes 8388612 | tf_op jit(solution)/shard_map/all_to_all | solution.py:28
  608.6 19.5 %multiply_reduce_fusion.2 = (f32[]{:T(128)}, f32[]{:T(128)}, f32[32,8,1024]{2,1,0:T(8,128)S(1)}) fusion(f32[32,8,1024]{2,1,0:T(8,128)S(1)} %copy-done.3, f32[2048,2,32,8]{0,3,1,2:T(8,128)} %all_to_all.76, f32[1024,1,2048]{2,0,1:T(8,128)} %get-tuple-element.20, f32[1024,1,2048]{2,0,1:T(8,128)} %get-tuple-element.21), kind=kOutput, calls=%fused_computation.111 | convolution fusion | flops 12894339072 | bytes 23068680 | tf_op jit(solution)/shard_map/fctl,kcf->tlk/dot_general | solution.py:31
  628.1 37.4 %all-reduce.1 = (f32[]{:T(128)}, f32[]{:T(128)}) all-reduce(f32[]{:T(128)} %get-tuple-element.5, f32[]{:T(128)} %get-tuple-element.4), channel_id=1, replica_groups=mesh['row'=4,'col'=8] {'row','col'}, use_global_device_ids=true, to_apply=%region_1.2 | all-reduce | flops 2 | bytes 16 | tf_op jit(solution)/shard_map/psum | solution.py:89
  667.1 21.2 %fusion.63 = bf16[2048,2,32,8]{0,2,3,1:T(8,128)(2,1)} fusion(f32[32,8,1024]{2,1,0:T(8,128)S(1)} %multiply_add_fusion.1, f32[1024,1,2048]{2,0,1:T(8,128)} %get-tuple-element.20, f32[1024,1,2048]{2,0,1:T(8,128)} %get-tuple-element.21), kind=kOutput, calls=%fused_computation.72 | convolution fusion | flops 12894339072 | bytes 19922944 | tf_op jit(solution)/shard_map/tlk,kcf->fctl/dot_general | solution.py:56
  698.2 12.2 %reshape.90 = bf16[32,2,16384]{2,1,0:T(2,128)(2,1)S(1)} reshape(bf16[2048,2,8,32]{3,2,1,0:T(8,128)(2,1)} %bitcast.202) | data formatting | bytes 4194304
  710.5 55.6 %all_to_all.91 = bf16[32,2,16384]{2,1,0:T(2,128)(2,1)} all-to-all(bf16[32,2,16384]{2,1,0:T(2,128)(2,1)S(1)} %reshape.90), channel_id=1, replica_groups=mesh['row'=4,'col'=8] {'row','col'}, dimensions={0} | all-to-all | bytes 4194304 | tf_op jit(solution)/shard_map/all_to_all | solution.py:59
  777.8 12.1 %copy.73 = bf16[32,64,2,32,8]{1,4,0,3,2:T(8,128)(2,1)} copy(bf16[32,64,2,32,8]{3,4,2,1,0:T(8,128)(2,1)} %bitcast.203) | data formatting | bytes 4194304 | tf_op jit(solution)/shard_map/all_to_all | solution.py:59
  797.3 12.7 %fusion.4 = f32[64,32,512]{2,1,0:T(8,128)} fusion(bf16[64,1,32,256]{3,2,0,1:T(8,128)(2,1)S(1)} %copy.90, bf16[64,2,512,256]{3,2,1,0:T(8,128)(2,1)} %param.6), kind=kOutput, calls=%fused_computation.5 | convolution fusion | flops 536870912 | bytes 22020096 | tf_op jit(solution)/shard_map/fml,ftl->ftm/dot_general | solution.py:73
  810.0 12.7 %fusion.26 = f32[64,32,512]{2,1,0:T(8,128)} fusion(bf16[64,1,32,256]{3,2,0,1:T(8,128)(2,1)S(1)} %copy.90, bf16[64,2,512,256]{3,2,1,0:T(8,128)(2,1)} %param.6), kind=kOutput, calls=%fused_computation.27 | convolution fusion | flops 536870912 | bytes 22020096 | tf_op jit(solution)/shard_map/fml,ftl->ftm/dot_general | solution.py:64
  825.8 12.7 %fusion.22 = f32[64,32,512]{2,1,0:T(8,128)} fusion(bf16[64,1,32,256]{3,2,0,1:T(8,128)(2,1)S(1)} %copy.91, bf16[64,2,512,256]{3,2,1,0:T(8,128)(2,1)} %param.6), kind=kOutput, calls=%fused_computation.23 | convolution fusion | flops 536870912 | bytes 22020096 | tf_op jit(solution)/shard_map/fml,ftl->ftm/dot_general | solution.py:70
  838.5 12.7 %fusion.6 = f32[64,32,512]{2,1,0:T(8,128)} fusion(bf16[64,1,32,256]{3,2,0,1:T(8,128)(2,1)S(1)} %copy.91, bf16[64,2,512,256]{3,2,1,0:T(8,128)(2,1)} %param.6), kind=kOutput, calls=%fused_computation.7 | convolution fusion | flops 536870912 | bytes 22020096 | tf_op jit(solution)/shard_map/fml,ftl->ftm/dot_general | solution.py:67
  875.1 12.8 %add_bitcast_fusion.1 = f32[64,1,32,256]{3,2,0,1:T(8,128)} fusion(f32[64,32,256]{2,1,0:T(8,128)} %fusion.2, f32[64,32,512]{2,1,0:T(8,128)} %fusion.26, f32[64,32,512]{2,1,0:T(8,128)} %fusion.6, f32[32,512]{1,0:T(8,128)S(1)} %get-tuple-element.10, bf16[64,1,32,256]{3,2,0,1:T(8,128)(2,1)S(1)} %copy.90, f32[64]{0:T(128)S(1)} %copy-done.9, ...), kind=kOutput, calls=%fused_computation.77 | convolution fusion | flops 542113792 | bytes 30474496 | tf_op jit(solution)/shard_map/fml,ftm->ftl/dot_general | solution.py:34
  887.9 13.1 %add_bitcast_fusion = f32[64,1,32,256]{3,2,0,1:T(8,128)} fusion(f32[64,32,256]{2,1,0:T(8,128)} %fusion, f32[64,32,512]{2,1,0:T(8,128)} %fusion.22, f32[64,32,512]{2,1,0:T(8,128)} %fusion.4, f32[32,512]{1,0:T(8,128)S(1)} %get-tuple-element.10, bf16[64,1,32,256]{3,2,0,1:T(8,128)(2,1)S(1)} %copy.91, f32[64]{0:T(128)S(1)} %copy-done.9, ...), kind=kOutput, calls=%fused_computation.76 | convolution fusion | flops 542113792 | bytes 30474496 | tf_op jit(solution)/shard_map/fml,ftm->ftl/dot_general | solution.py:40
  924.0 98.5 %all_to_all.92 = f32[32,1,32768]{2,1,0:T(1,128)} all-to-all(f32[32,1,32768]{2,1,0:T(1,128)} %reshape.92), channel_id=1, replica_groups=mesh['row'=4,'col'=8] {'row','col'}, dimensions={0} | all-to-all | bytes 8388608 | tf_op jit(solution)/shard_map/all_to_all | solution.py:28
  1022.5 13.8 %reduce.2 = f32[32,32768]{1,0:T(8,128)} reduce(f32[32,1,32768]{2,1,0:T(1,128)} %all_to_all.92, f32[]{:T(128)} %broadcast.90), dimensions={1}, to_apply=%all_to_all.81.reduce_sub_computation | reduce | bytes 8388612 | tf_op jit(solution)/shard_map/all_to_all | solution.py:28
  1063.1 19.6 %multiply_reduce_fusion = (f32[]{:T(128)}, f32[]{:T(128)}, f32[32,8,1024]{2,1,0:T(8,128)}) fusion(f32[32,8,1024]{2,1,0:T(8,128)S(1)} %copy-done.8, f32[32,8,1024]{2,1,0:T(8,128)S(1)} %copy-done.4, f32[32,8,1024]{2,1,0:T(8,128)S(1)} %copy-done.6, f32[]{:T(128)S(6)} %div.14, f32[2048,2,32,8]{0,3,1,2:T(8,128)} %all_to_all.84, ...), kind=kOutput, calls=%fused_computation.107 | convolution fusion | flops 12894863360 | bytes 25165836 | tf_op jit(solution)/shard_map/fctl,kcf->tlk/dot_general | solution.py:31
  1082.7 38.0 %all-reduce = (f32[]{:T(128)}, f32[]{:T(128)}) all-reduce(f32[]{:T(128)} %get-tuple-element.3, f32[]{:T(128)} %get-tuple-element.2), channel_id=1, replica_groups=mesh['row'=4,'col'=8] {'row','col'}, use_global_device_ids=true, to_apply=%region_5.6 | all-reduce | flops 2 | bytes 16 | tf_op jit(solution)/shard_map/psum | solution.py:89
  (63 shorter events, 306.2 us)
Async XLA Ops:
  54.3 102.8 %all-to-all-start = ((f32[32,1,32768]{2,1,0:T(1,128)}), f32[32,1,32768]{2,1,0:T(1,128)}, u32[]{:S(2)}, u32[]{:S(2)}) async-start(f32[32,1,32768]{2,1,0:T(1,128)} %reshape.84), calls=%async_computation | async-start | bytes 8388608 | tf_op jit(solution)/shard_map/all_to_all | solution.py:28
  216.8 1.0 copy-start.2
  408.3 11.9 %copy-start.9 = (f32[64]{0:T(128)S(1)}, f32[64]{0:T(128)}, u32[]{:S(2)}) copy-start(f32[64]{0:T(128)} %param.10) | copy-start | bytes 772
  433.0 13.3 %copy-start.1 = (f32[64,1,32,256]{3,2,0,1:T(8,128)S(1)}, f32[64,1,32,256]{3,2,0,1:T(8,128)}, u32[]{:S(2)}) copy-start(f32[64,1,32,256]{3,2,0,1:T(8,128)} %add_bitcast_fusion.3) | copy-start | bytes 6291460
  469.4 98.7 %all-to-all-start.2 = ((f32[32,1,32768]{2,1,0:T(1,128)}), f32[32,1,32768]{2,1,0:T(1,128)}, u32[]{:S(2)}, u32[]{:S(2)}) async-start(f32[32,1,32768]{2,1,0:T(1,128)} %reshape.88), calls=%async_computation.2 | async-start | bytes 8388608 | tf_op jit(solution)/shard_map/all_to_all | solution.py:28
  600.7 7.9 copy-start.3
  628.1 60.2 %copy-start.5 = (f32[32,8,1024]{2,1,0:T(8,128)}, f32[32,8,1024]{2,1,0:T(8,128)S(1)}, u32[]{:S(2)}) copy-start(f32[32,8,1024]{2,1,0:T(8,128)S(1)} %get-tuple-element.18) | copy-start | bytes 3145732
  667.1 21.2 %copy-start.7 = (f32[32,8,1024]{2,1,0:T(8,128)}, f32[32,8,1024]{2,1,0:T(8,128)S(1)}, u32[]{:S(2)}) copy-start(f32[32,8,1024]{2,1,0:T(8,128)S(1)} %multiply_add_fusion.1) | copy-start | bytes 3145732
  887.9 13.1 %copy-start = (f32[64,1,32,256]{3,2,0,1:T(8,128)S(1)}, f32[64,1,32,256]{3,2,0,1:T(8,128)}, u32[]{:S(2)}) copy-start(f32[64,1,32,256]{3,2,0,1:T(8,128)} %add_bitcast_fusion.1) | copy-start | bytes 6291460
  1055.1 8.0 copy-start.4
  1055.1 8.0 copy-start.6
  1055.1 8.0 copy-start.8
where the time goes:
time: 1130 us
  matrix products  329 us (29%)
  blocking collectives  283 us (25%)
  local copies, waits for them, and re-layouts  250 us (22%)
  waiting for transfers between devices  155 us (14%)
  other arithmetic  93.1 us (8%)
    all_to_all x2, waiting for transfers between devices, to_taps(): lax.all_to_all(spectrum, ('row', 'col'), split_axis=3, concat_axis=0, til...  155 us
    unnamed x34, local copies, waits for them, and re-layouts  112 us
    all_to_all x2, blocking collectives, body(): lax.all_to_all(to_spectrum, ('row', 'col'), split_axis=0, concat_axis=3,...  109 us
    all_to_all x1, blocking collectives, to_taps(): lax.all_to_all(spectrum, ('row', 'col'), split_axis=3, concat_axis=0, til...  98.5 us
    psum x2, blocking collectives, body(): lax.psum((along_term, jnp.sum(direction * image_taps)), ('row', 'col'))  75.5 us
    all_to_all x7, local copies, waits for them, and re-layouts, to_taps(): lax.all_to_all(spectrum, ('row', 'col'), split_axis=3, concat_axis=0, til...  58.6 us
    dot_general x3, matrix products, to_taps(): jnp.einsum('fctl,kcf->tlk', regrouped, dft_table, precision=lax.Precision...  57.9 us
    all_to_all x3, other arithmetic, to_taps(): lax.all_to_all(spectrum, ('row', 'col'), split_axis=3, concat_axis=0, til...  41.3 us
  transfers between devices with their start and end apart: 2, of which 2 were waited for; matrix products, arithmetic and copies ran while one was open for 3% of the time, Pallas kernels for 0%

commit v1 on v0

v1 whole, which is shorter than its diff:
```python
import math

import jax
import jax.numpy as jnp
from jax import lax
from jax.experimental import pallas as pl
from jax.experimental.pallas import tpu as pltpu
from jax.sharding import PartitionSpec as P

K = 1024
F = 2048
ITERS = 2
AXES = ("row", "col")
BF16 = jnp.bfloat16
F32 = jnp.float32
NT = (((1,), (1,)), ((), ()))
VMEM_BYTES = 60 * 2**20


def dot_nn(a, b):
    return jnp.dot(a, b, preferred_element_type=F32)


def dot_nt(a, b):
    return lax.dot_general(a, b, NT, preferred_element_type=F32)


def build_table(taps, bins):
    tap_index = jnp.arange(taps, dtype=jnp.int32)[:, None]
    bin_index = jnp.arange(bins, dtype=jnp.int32)[None, :]
    phase = (tap_index * bin_index % bins).astype(jnp.float32) * (2.0 * math.pi / bins)
    return jnp.stack([jnp.cos(phase), -jnp.sin(phase)], axis=1) / math.sqrt(bins)


def plain_body(transfer, target, zone_mask, dark_weight, reg_weight, momentum):
    dft_table = build_table(K, F)
    mic_gains = jnp.where(zone_mask == 1, jnp.float32(1.0), dark_weight[:, None])
    weight_real = transfer[:, 0]
    weight_imag = transfer[:, 1]
    reg_term = reg_weight[:, None, None]

    def to_taps(spectrum):
        regrouped = lax.all_to_all(spectrum, AXES, split_axis=3, concat_axis=0, tiled=True)
        return jnp.einsum("fctl,kcf->tlk", regrouped, dft_table, precision=lax.Precision.HIGHEST)

    def contract(spec, first, second):
        return jnp.einsum(spec, first, second, preferred_element_type=jnp.float32)

    def back_project(err_real, err_imag):
        spec = "fml,ftm->ftl"
        back_real = contract(spec, weight_real, err_real) + contract(spec, weight_imag, err_imag)
        back_imag = contract(spec, weight_real, err_imag) - contract(spec, weight_imag, err_real)
        return back_real, back_imag

    rhs_error = jnp.where(zone_mask[None, None] == 1, target, jnp.zeros_like(target))
    rhs = to_taps(jnp.stack(back_project(rhs_error[:, 0], rhs_error[:, 1]), axis=1))
    filters = jnp.zeros_like(rhs)
    residual = rhs
    direction = rhs
    for iteration in range(ITERS):
        along_term = jnp.sum(residual * direction)
        to_spectrum = jnp.einsum(
            "tlk,kcf->fctl", direction, dft_table, precision=lax.Precision.HIGHEST
        ).astype(jnp.bfloat16)
        spec = lax.all_to_all(to_spectrum, AXES, split_axis=0, concat_axis=3, tiled=True)
        spec_real = spec[:, 0]
        spec_imag = spec[:, 1]
        form = "fml,ftl->ftm"
        press_real = contract(form, weight_real, spec_real) - contract(form, weight_imag, spec_imag)
        press_imag = contract(form, weight_real, spec_imag) + contract(form, weight_imag, spec_real)
        back_real, back_imag = back_project(
            (mic_gains * press_real).astype(jnp.bfloat16),
            (mic_gains * press_imag).astype(jnp.bfloat16),
        )
        image_taps = to_taps(
            jnp.stack(
                [
                    back_real + reg_term * spec_real.astype(jnp.float32),
                    back_imag + reg_term * spec_imag.astype(jnp.float32),
                ],
                axis=1,
            )
        )
        along_sum, bend_sum = lax.psum((along_term, jnp.sum(direction * image_taps)), AXES)
        step_size = along_sum / bend_sum
        filters = filters + step_size * direction
        residual = residual - step_size * image_taps
        if iteration + 1 < ITERS:
            direction = residual + momentum[iteration] * direction
    return (filters, residual)


def split_table(devices, bins, taps):
    local = bins // devices
    tap = jnp.arange(taps, dtype=jnp.int32)
    scale = 2.0 * math.pi / bins
    coarse = (jnp.arange(devices, dtype=jnp.int32)[:, None] * local * tap[None, :]) % bins
    fine = (jnp.arange(local, dtype=jnp.int32)[:, None] * tap[None, :]) % bins
    coarse = coarse.astype(F32) * scale
    fine = fine.astype(F32) * scale
    norm = 1.0 / math.sqrt(bins)
    cos_c, sin_c = (jnp.cos(coarse) * norm)[:, None], (jnp.sin(coarse) * norm)[:, None]
    cos_f, sin_f = jnp.cos(fine)[None], jnp.sin(fine)[None]
    cos_c, sin_c, cos_f, sin_f = lax.optimization_barrier((cos_c, sin_c, cos_f, sin_f))
    table = jnp.stack([cos_c * cos_f - sin_c * sin_f, -(sin_c * cos_f + cos_c * sin_f)], axis=1)
    high = lax.reduce_precision(table, 8, 7)
    shape = (2 * bins, taps)
    return high.astype(BF16).reshape(shape), (table - high).astype(BF16).reshape(shape)


LANES = 128


def turn_out(turn_ref, out_ref, targets):
    devices, _, width = out_ref.shape
    step_rows = targets * width
    blocks = turn_ref.shape[0] // step_rows
    each = devices // blocks

    def step(pair, carry):
        for block in range(blocks):
            halves = []
            for side in range(2):
                start = block * step_rows + (2 * pair + side) * width
                halves.append(turn_ref[pl.ds(start, width), :].T.reshape(each, 8, width))
            both = jnp.concatenate(halves, axis=1).astype(BF16)
            out_ref[block * each : (block + 1) * each, pl.ds(16 * pair, 16), :] = both
        return carry

    lax.fori_loop(0, targets // 2, step, 0)


def turn_in(in_ref, turn_ref, targets):
    devices, _, width = in_ref.shape
    step_rows = targets * width
    blocks = turn_ref.shape[0] // step_rows
    each = devices // blocks

    def step(pair, carry):
        for block in range(blocks):
            part = in_ref[block * each : (block + 1) * each, pl.ds(16 * pair, 16), :].astype(F32)
            for side in range(2):
                half = part[:, 8 * side : 8 * side + 8, :].reshape(LANES, width)
                start = block * step_rows + (2 * pair + side) * width
                turn_ref[pl.ds(start, width), :] = half.T
        return carry

    lax.fori_loop(0, targets // 2, step, 0)


def load_bin(turn_ref, row, targets, stride):
    step_rows = targets * stride
    return jnp.concatenate(
        [
            turn_ref[pl.ds(block * step_rows + row, targets, stride=stride), :]
            for block in range(turn_ref.shape[0] // step_rows)
        ],
        axis=1,
    )


def store_bin(turn_ref, row, targets, stride, values):
    step_rows = targets * stride
    for block in range(turn_ref.shape[0] // step_rows):
        part = values[:, block * LANES : (block + 1) * LANES]
        turn_ref[pl.ds(block * step_rows + row, targets, stride=stride), :] = part


def store_sums(out_ref, along, bend):
    row = lax.broadcasted_iota(jnp.int32, along.shape, 0)
    value = jnp.where(row < 3, along, bend)
    first = value.astype(BF16).astype(F32)
    second = (value - first).astype(BF16).astype(F32)
    third = value - first - second
    term = jnp.where(row % 3 == 0, first, jnp.where(row % 3 == 1, second, third))
    term = jnp.where(row < 6, term, 0.0).astype(BF16)
    rows = out_ref.shape[1]
    out_ref[:, rows - 8 : rows, :] = jnp.broadcast_to(term[None], (out_ref.shape[0],) + term.shape)


def step_of(back_ref):
    rows = back_ref.shape[1]
    sums = jnp.sum(back_ref[:, rows - 8 : rows, :].astype(F32), axis=0)
    along = sums[0:1, 0:1] + sums[1:2, 0:1] + sums[2:3, 0:1]
    bend = sums[3:4, 0:1] + sums[4:5, 0:1] + sums[5:6, 0:1]
    return along / bend


def back_of(err, weight, half):
    turned = jnp.concatenate([err[half:], -err[:half]], axis=0)
    return dot_nn(err, weight[0]) + dot_nn(turned, weight[1])


GROUP = 8


def start_weights(w_hbm, w_buf, sems):
    groups = w_buf.shape[0] // GROUP
    copies = [
        pltpu.make_async_copy(
            w_hbm.at[pl.ds(g * GROUP, GROUP)], w_buf.at[pl.ds(g * GROUP, GROUP)], sems.at[g]
        )
        for g in range(groups)
    ]
    for copy in copies:
        copy.start()


def wait_weights(w_hbm, w_buf, sems, g):
    pltpu.make_async_copy(
        w_hbm.at[pl.ds(g * GROUP, GROUP)], w_buf.at[pl.ds(g * GROUP, GROUP)], sems.at[g]
    ).wait()


def rhs_kernel(target_ref, mask_ref, w_hbm, out_ref, w_buf, back_buf, sems):
    bins, _, targets, mics = target_ref.shape
    start_weights(w_hbm, w_buf, sems)
    bright = mask_ref[...] == 1
    bright = jnp.concatenate([bright, bright], axis=0)

    def group(g, carry):
        wait_weights(w_hbm, w_buf, sems, g)
        for b in range(GROUP):
            j = g * GROUP + b
            wanted = target_ref[j].reshape(2 * targets, mics).astype(F32)
            err = jnp.where(bright, wanted, 0.0).astype(BF16)
            back = back_of(err, w_buf.at[j], targets)
            store_bin(back_buf, j, targets, 2 * bins, back[:targets])
            store_bin(back_buf, bins + j, targets, 2 * bins, back[targets:])
        return carry

    lax.fori_loop(0, bins // GROUP, group, 0)
    turn_out(back_buf, out_ref, targets)


def normal_kernel(
    spec_ref, mask_ref, dark_ref, reg_ref, along_ref, w_hbm,
    out_ref, w_buf, spec_buf, back_buf, sems,
):
    bins = w_buf.shape[0]
    targets = mask_ref.shape[0]
    start_weights(w_hbm, w_buf, sems)
    gains = jnp.where(mask_ref[...] == 1, jnp.float32(1.0), dark_ref[...])
    gains = jnp.concatenate([gains, gains], axis=0)
    turn_in(spec_ref, spec_buf, targets)

    def group(g, bend):
        wait_weights(w_hbm, w_buf, sems, g)
        for b in range(GROUP):
            j = g * GROUP + b
            weight = w_buf.at[j]
            real = load_bin(spec_buf, j, targets, 2 * bins)
            imag = load_bin(spec_buf, bins + j, targets, 2 * bins)
            wide = jnp.concatenate([real, imag], axis=0)
            spec = wide.astype(BF16)
            turned = jnp.concatenate([-imag, real], axis=0).astype(BF16)
            press = dot_nt(spec, weight[0]) + dot_nt(turned, weight[1])
            back = back_of((gains * press).astype(BF16), weight, targets)
            back = back + reg_ref[j] * wide
            bend = bend + wide * back
            store_bin(back_buf, j, targets, 2 * bins, back[:targets])
            store_bin(back_buf, bins + j, targets, 2 * bins, back[targets:])
        return bend

    bend = lax.fori_loop(0, bins // GROUP, group, jnp.zeros((2 * targets, w_buf.shape[3]), F32))
    turn_out(back_buf, out_ref, targets)
    store_sums(out_ref, along_ref[...], jnp.sum(bend))


CHUNK = 8


def start_table(high_hbm, low_hbm, high_buf, low_buf, sems):
    rows = high_buf.shape[0] // 4
    for c in range(4):
        part = pl.ds(c * rows, rows)
        pltpu.make_async_copy(high_hbm.at[part], high_buf.at[part], sems.at[0, c]).start()
        pltpu.make_async_copy(low_hbm.at[part], low_buf.at[part], sems.at[1, c]).start()


def taps_of(back_ref, count, high_hbm, low_hbm, high_buf, low_buf, sems):
    rows = high_buf.shape[0] // 4
    per = back_ref.shape[0] // 4
    total = None
    for c in range(4):
        part = pl.ds(c * rows, rows)
        pltpu.make_async_copy(high_hbm.at[part], high_buf.at[part], sems.at[0, c]).wait()
        pltpu.make_async_copy(low_hbm.at[part], low_buf.at[part], sems.at[1, c]).wait()
        block = jnp.concatenate([back_ref[c * per + d, :count, :] for d in range(per)], axis=1)
        term = dot_nn(block, high_buf[part, :]) + dot_nn(block, low_buf[part, :])
        total = term if total is None else total + term
    return total


def spectrum_to(out_ref, direction, high_buf, low_buf):
    rows = high_buf.shape[0] // 4
    per = out_ref.shape[0] // 4
    width = out_ref.shape[2]
    count = direction.shape[0]
    high = direction.astype(BF16)
    low = (direction - high.astype(F32)).astype(BF16)
    both = jnp.concatenate([high, low], axis=0)
    for c in range(4):
        part = pl.ds(c * rows, rows)
        wide = dot_nt(both, high_buf[part, :])
        spec = wide[:count] + wide[count:] + dot_nt(high, low_buf[part, :])
        for d in range(per):
            out_ref[c * per + d] = spec[:, d * width : (d + 1) * width].astype(BF16)


def first_kernel(
    back_ref, high_hbm, low_hbm, rhs_ref, spec_ref, along_ref, high_buf, low_buf, sems
):
    start_table(high_hbm, low_hbm, high_buf, low_buf, sems)
    rhs = taps_of(back_ref, rhs_ref.shape[0], high_hbm, low_hbm, high_buf, low_buf, sems)
    rhs_ref[...] = rhs
    along_ref[...] = jnp.broadcast_to(jnp.sum(rhs * rhs), along_ref.shape)
    spectrum_to(spec_ref, rhs, high_buf, low_buf)


def middle_kernel(
    back_ref, rhs_ref, momentum_ref, high_hbm, low_hbm,
    filters_ref, residual_ref, direction_ref, spec_ref, along_ref, high_buf, low_buf, sems,
):
    start_table(high_hbm, low_hbm, high_buf, low_buf, sems)
    step = step_of(back_ref)
    image = taps_of(back_ref, residual_ref.shape[0], high_hbm, low_hbm, high_buf, low_buf, sems)
    rhs = rhs_ref[...]
    residual = rhs - step * image
    direction = residual + momentum_ref[0] * rhs
    filters_ref[...] = step * rhs
    residual_ref[...] = residual
    direction_ref[...] = direction
    along_ref[...] = jnp.broadcast_to(jnp.sum(residual * direction), along_ref.shape)
    spectrum_to(spec_ref, direction, high_buf, low_buf)


def last_kernel(
    back_ref, filters_ref, residual_ref, direction_ref, high_hbm, low_hbm,
    filters_out, residual_out, high_buf, low_buf, sems,
):
    start_table(high_hbm, low_hbm, high_buf, low_buf, sems)
    step = step_of(back_ref)
    image = taps_of(back_ref, residual_ref.shape[0], high_hbm, low_hbm, high_buf, low_buf, sems)
    filters_out[...] = filters_ref[...] + step * direction_ref[...]
    residual_out[...] = residual_ref[...] - step * image


def vmem():
    return pl.BlockSpec(memory_space=pltpu.VMEM)


def smem():
    return pl.BlockSpec(memory_space=pltpu.SMEM)


def hbm():
    return pl.BlockSpec(memory_space=pl.ANY)


def kernel_body(transfer, target, zone_mask, dark_weight, reg_weight, momentum):
    bins, _, mics, speakers = transfer.shape
    targets = target.shape[2]
    devices = F // bins
    rows = targets * (speakers // devices)
    block = jax.ShapeDtypeStruct((devices, rows, 2 * bins), BF16)
    summed = jax.ShapeDtypeStruct((devices, rows + 8, 2 * bins), BF16)
    tile = jax.ShapeDtypeStruct((8, 128), F32)
    taps = jax.ShapeDtypeStruct((rows, K), F32)
    params = pltpu.CompilerParams(vmem_limit_bytes=VMEM_BYTES)
    high, low = split_table(devices, F, K)
    dark = dark_weight[:, None]
    bin_scratch = [
        pltpu.VMEM((speakers // LANES * targets * 2 * bins, LANES), F32),
        pltpu.SemaphoreType.DMA((bins // GROUP,)),
    ]
    weights = pltpu.VMEM(transfer.shape, BF16)
    table_scratch = [
        pltpu.VMEM(high.shape, BF16),
        pltpu.VMEM(low.shape, BF16),
        pltpu.SemaphoreType.DMA((2, 4)),
    ]

    def exchange(payload):
        return lax.all_to_all(payload, AXES, split_axis=0, concat_axis=0, tiled=True)

    def normal(spec, along):
        return pl.pallas_call(
            normal_kernel,
            in_specs=[vmem(), vmem(), vmem(), smem(), vmem(), hbm()],
            out_specs=vmem(),
            out_shape=summed,
            scratch_shapes=[weights, bin_scratch[0]] + bin_scratch,
            compiler_params=params,
            name="normal",
        )(spec, zone_mask, dark, reg_weight, along, transfer)

    back = pl.pallas_call(
        rhs_kernel,
        in_specs=[vmem(), vmem(), hbm()],
        out_specs=vmem(),
        out_shape=block,
        scratch_shapes=[weights] + bin_scratch,
        compiler_params=params,
        name="rhs_back",
    )(target, zone_mask, transfer)
    rhs, spec, along = pl.pallas_call(
        first_kernel,
        in_specs=[vmem(), hbm(), hbm()],
        out_specs=[vmem(), vmem(), vmem()],
        out_shape=[taps, block, tile],
        scratch_shapes=table_scratch,
        compiler_params=params,
        name="first_taps",
    )(exchange(back), high, low)
    back = normal(exchange(spec), along)
    filters, residual, direction, spec, along = pl.pallas_call(
        middle_kernel,
        in_specs=[vmem(), vmem(), smem(), hbm(), hbm()],
        out_specs=[vmem()] * 5,
        out_shape=[taps, taps, taps, block, tile],
        scratch_shapes=table_scratch,
        compiler_params=params,
        name="middle_taps",
    )(exchange(back), rhs, momentum, high, low)
    back = normal(exchange(spec), along)
    filters, residual = pl.pallas_call(
        last_kernel,
        in_specs=[vmem()] * 4 + [hbm(), hbm()],
        out_specs=[vmem(), vmem()],
        out_shape=[taps, taps],
        scratch_shapes=table_scratch,
        compiler_params=params,
        name="last_taps",
    )(exchange(back), filters, residual, direction, high, low)
    shape = (targets, speakers // devices, K)
    return filters.reshape(shape), residual.reshape(shape)


def body(transfer, target, *rest):
    bins, _, mics, speakers = transfer.shape
    devices = F // bins
    whole_tiles = (
        bins == 64
        and speakers == 8 * devices
        and speakers % 128 == 0
        and mics % 128 == 0
        and target.shape[2] == 32
        and devices % 4 == 0
    )
    return (kernel_body if whole_tiles else plain_body)(transfer, target, *rest)


def solution(mesh):
    in_specs = (
        P(AXES, None, None, None),
        P(AXES, None, None, None),
        P(),
        P(),
        P(AXES),
        P(),
    )
    out_specs = (P(None, AXES, None), P(None, AXES, None))
    return jax.shard_map(body, mesh=mesh, in_specs=in_specs, out_specs=out_specs, check_vma=False)
```

time: 1130 us -> 402 us (0.36)
  matrix products: 329 us -> 0 us
  local copies, waits for them, and re-layouts: 250 us -> 4.69 us
  blocking collectives: 283 us -> 109 us
  Pallas kernels: 0 us -> 123 us
  other arithmetic: 93.1 us -> 14.7 us
  waiting for transfers between devices: 155 us -> 136 us
    dot_general x25 -> x0, matrix products: 329 us -> none  [the longest x3 57.9 us: to_taps(): jnp.einsum('fctl,kcf->tlk', regrouped, dft_table, precision=lax.Precision...]
    pallas_call x0 -> x6, Pallas kernels: none -> 123 us  [the longest x2 60.8 us: normal(): pl.pallas_call(normal_kernel, in_specs=[vmem(), vmem(), vmem(), smem(), v...]
    unnamed x34 -> x8, local copies, waits for them, and re-layouts: 112 us -> 4 us
    all_to_all x3 -> x2, blocking collectives: 207 us -> 109 us  [exchange(): lax.all_to_all(payload, AXES, split_axis=0, concat_axis=0, tiled=True)]
    all_to_all x9 -> x0, local copies, waits for them, and re-layouts: 82.9 us -> none  [the longest x7 58.6 us: to_taps(): lax.all_to_all(spectrum, ('row', 'col'), split_axis=3, concat_axis=0, til...]
    psum x2 -> x0, blocking collectives: 75.5 us -> none  [body(): lax.psum((along_term, jnp.sum(direction * image_taps)), ('row', 'col'))]
    all_to_all x3 -> x0, other arithmetic: 41.3 us -> none  [to_taps(): lax.all_to_all(spectrum, ('row', 'col'), split_axis=3, concat_axis=0, til...]
    neg x1 -> x0, other arithmetic: 34.6 us -> none  [build_table(): -jnp.sin(phase)]
  transfers between devices with their start and end apart: 2 -> 3, of which waited for: 2 -> 3; matrix products, arithmetic and copies ran while one was open for 3% -> 4% of each run, Pallas kernels for 0% -> 0%
where the time goes in v1:
time: 402 us
  waiting for transfers between devices  136 us (34%)
  Pallas kernels  123 us (31%)
  blocking collectives  109 us (27%)
  other arithmetic  14.7 us (4%)
  starting transfers between devices  13.8 us (3%)
  local copies, waits for them, and re-layouts  4.69 us (1%)
    all_to_all x3, waiting for transfers between devices, exchange(): lax.all_to_all(payload, AXES, split_axis=0, concat_axis=0, tiled=True)  136 us
    all_to_all x2, blocking collectives, exchange(): lax.all_to_all(payload, AXES, split_axis=0, concat_axis=0, tiled=True)  109 us
    pallas_call x2, Pallas kernels, normal(): pl.pallas_call(normal_kernel, in_specs=[vmem(), vmem(), vmem(), smem(), v...  60.8 us
    pallas_call x1, Pallas kernels, kernel_body(): pl.pallas_call(middle_kernel, in_specs=[vmem(), vmem(), smem(), hbm(), hb...  17.1 us
    pallas_call x1, Pallas kernels, kernel_body(): pl.pallas_call(rhs_kernel, in_specs=[vmem(), vmem(), hbm()], out_specs=vm...  17 us
    pallas_call x1, Pallas kernels, kernel_body(): pl.pallas_call(first_kernel, in_specs=[vmem(), hbm(), hbm()], out_specs=[...  16.6 us
    all_to_all x3, starting transfers between devices, exchange(): lax.all_to_all(payload, AXES, split_axis=0, concat_axis=0, tiled=True)  13.8 us
    pallas_call x1, Pallas kernels, kernel_body(): pl.pallas_call(last_kernel, in_specs=[vmem()] * 4 + [hbm(), hbm()], out_s...  11 us
  transfers between devices with their start and end apart: 3, of which 3 were waited for; matrix products, arithmetic and copies ran while one was open for 4% of the time, Pallas kernels for 0%

profile of v1, /device:TPU:0, one launch (start us, length us, event | category | flops | bytes accessed | tf_op | source)
XLA Modules:
  0.0 401.6 jit_solution(14863746142573323962)
XLA Ops:
  0.6 17.0 %rhs_back.1 = bf16[32,256,128]{2,1,0:T(8,128)(2,1)} custom-call(bf16[64,2,32,512]{3,2,1,0:T(8,128)(2,1)} %target_ref.1, s32[32,512]{1,0:T(8,128)} %mask_ref.5, bf16[64,2,512,256]{3,2,1,0:T(8,128)(2,1)} %w_hbm.5), custom_call_target="tpu_custom_call" | custom-call | tf_op jit(solution)/shard_map/rhs_back/pallas_call | solution.py:398
  17.7 7.3 %all-to-all-start = ((bf16[32,256,128]{2,1,0:T(8,128)(2,1)}), bf16[32,256,128]{2,1,0:T(8,128)(2,1)S(1)}, u32[]{:S(2)}, u32[]{:S(2)}) async-start(bf16[32,256,128]{2,1,0:T(8,128)(2,1)} %rhs_back.1), calls=%async_computation | async-start | bytes 4194304 | tf_op jit(solution)/shard_map/all_to_all | solution.py:385
  25.0 1.0 fusion.10
  26.0 0.6 sine_multiply_fusion
  26.6 2.5 multiply_subtract_fusion
  29.1 2.4 pad_maximum_fusion
  31.5 8.2 %fusion = (bf16[4096,1024]{1,0:T(8,128)(2,1)}, bf16[4096,1024]{1,0:T(8,128)(2,1)}) fusion(f32[32,2,64,1024]{3,2,1,0:T(8,128)S(1)} %pad_maximum_fusion), kind=kLoop, calls=%fused_computation.2 | loop fusion | flops 16777216 | bytes 33554432 | tf_op jit(solution)/shard_map/convert_element_type | solution.py:108
  39.7 35.3 %all-to-all-done.back_ref = bf16[32,256,128]{2,1,0:T(8,128)(2,1)S(1)} async-done(((bf16[32,256,128]{2,1,0:T(8,128)(2,1)}), bf16[32,256,128]{2,1,0:T(8,128)(2,1)S(1)}, u32[]{:S(2)}, u32[]{:S(2)}) %all-to-all-start) | async-done | bytes 2097184 | tf_op jit(solution)/shard_map/all_to_all | solution.py:385
  75.0 0.0 copy-start.1
  75.0 1.3 copy-done.1
  76.4 0.0 copy-start.3
  76.4 16.6 %first_taps.1 = (f32[256,1024]{1,0:T(8,128)}, bf16[32,256,128]{2,1,0:T(8,128)(2,1)}, f32[8,128]{1,0:T(8,128)}) custom-call(bf16[32,256,128]{2,1,0:T(8,128)(2,1)} %copy-done.1, bf16[4096,1024]{1,0:T(8,128)(2,1)} %get-tuple-element.31.high_hbm, bf16[4096,1024]{1,0:T(8,128)(2,1)} %get-tuple-element.30.low_hbm), custom_call_target="tpu_custom_call" | custom-call | tf_op jit(solution)/shard_map/first_taps/pallas_call | solution.py:407
  93.0 3.3 all-to-all-start.1
  96.3 0.0 copy-done.3
  96.3 0.7 copy.8.dark_ref
  97.0 49.4 %all-to-all-done.1.spec_ref = bf16[32,256,128]{2,1,0:T(8,128)(2,1)S(1)} async-done(((bf16[32,256,128]{2,1,0:T(8,128)(2,1)}), bf16[32,256,128]{2,1,0:T(8,128)(2,1)S(1)}, u32[]{:S(2)}, u32[]{:S(2)}) %all-to-all-start.1) | async-done | bytes 2097184 | tf_op jit(solution)/shard_map/all_to_all | solution.py:385
  146.3 0.0 copy-start.2
  146.3 1.3 copy-done.2
  147.6 30.4 %normal.2 = bf16[32,264,128]{2,1,0:T(8,128)(2,1)} custom-call(bf16[32,256,128]{2,1,0:T(8,128)(2,1)} %copy-done.2, s32[32,512]{1,0:T(8,128)} %mask_ref.5, f32[32,1]{1,0:T(8,128)} %copy.8.dark_ref, f32[64]{0:T(128)} %reg_ref.3, f32[8,128]{1,0:T(8,128)} %get-tuple-element.21.along_ref, bf16[64,2,512,256]{3,2,1,0:T(8,128)(2,1)} %w_hbm.5), custom_call_target="tpu_custom_call" | custom-call | tf_op jit(solution)/shard_map/normal/pallas_call | solution.py:388
  178.1 3.3 all-to-all-start.2
  182.0 50.9 %all-to-all-done.2.back_ref = bf16[32,264,128]{2,1,0:T(8,128)(2,1)S(1)} async-done(((bf16[32,264,128]{2,1,0:T(8,128)(2,1)}), bf16[32,264,128]{2,1,0:T(8,128)(2,1)S(1)}, u32[]{:S(2)}, u32[]{:S(2)}) %all-to-all-start.2) | async-done | bytes 2162720 | tf_op jit(solution)/shard_map/all_to_all | solution.py:385
  232.8 0.0 copy-start
  232.9 1.4 copy-done
  234.2 17.1 %middle_taps.1 = (f32[256,1024]{1,0:T(8,128)}, f32[256,1024]{1,0:T(8,128)}, f32[256,1024]{1,0:T(8,128)}, bf16[32,256,128]{2,1,0:T(8,128)(2,1)}, f32[8,128]{1,0:T(8,128)}) custom-call(bf16[32,264,128]{2,1,0:T(8,128)(2,1)} %copy-done, f32[256,1024]{1,0:T(8,128)} %get-tuple-element.22.rhs_ref, f32[1]{0:T(128)S(6)} %copy.10.momentum_ref, ...), custom_call_target="tpu_custom_call" | custom-call | tf_op jit(solution)/shard_map/middle_taps/pallas_call | solution.py:417
  251.3 53.5 %all_to_all.25.spec_ref = bf16[32,256,128]{2,1,0:T(8,128)(2,1)} all-to-all(bf16[32,256,128]{2,1,0:T(8,128)(2,1)} %get-tuple-element.23), channel_id=1, replica_groups=mesh['row'=4,'col'=8] {'row','col'}, dimensions={0} | all-to-all | bytes 4194304 | tf_op jit(solution)/shard_map/all_to_all | solution.py:385
  304.8 30.4 %normal.3 = bf16[32,264,128]{2,1,0:T(8,128)(2,1)} custom-call(bf16[32,256,128]{2,1,0:T(8,128)(2,1)} %all_to_all.25.spec_ref, s32[32,512]{1,0:T(8,128)} %mask_ref.5, f32[32,1]{1,0:T(8,128)} %copy.8.dark_ref, f32[64]{0:T(128)} %reg_ref.3, f32[8,128]{1,0:T(8,128)} %get-tuple-element.24.along_ref, bf16[64,2,512,256]{3,2,1,0:T(8,128)(2,1)} %w_hbm.5), custom_call_target="tpu_custom_call" | custom-call | tf_op jit(solution)/shard_map/normal/pallas_call | solution.py:388
  335.2 55.2 %all_to_all.26.back_ref = bf16[32,264,128]{2,1,0:T(8,128)(2,1)} all-to-all(bf16[32,264,128]{2,1,0:T(8,128)(2,1)} %normal.3), channel_id=1, replica_groups=mesh['row'=4,'col'=8] {'row','col'}, dimensions={0} | all-to-all | bytes 4325376 | tf_op jit(solution)/shard_map/all_to_all | solution.py:385
  390.4 11.0 %last_taps.1 = (f32[256,1024]{1,0:T(8,128)}, f32[256,1024]{1,0:T(8,128)}) custom-call(bf16[32,264,128]{2,1,0:T(8,128)(2,1)} %all_to_all.26.back_ref, f32[256,1024]{1,0:T(8,128)} %get-tuple-element.25.filters_ref, f32[256,1024]{1,0:T(8,128)} %get-tuple-element.26.residual_ref, f32[256,1024]{1,0:T(8,128)} %get-tuple-element.27.direction_ref, ...), custom_call_target="tpu_custom_call" | custom-call | tf_op jit(solution)/shard_map/last_taps/pallas_call | solution.py:427
  (1 shorter events, 0.0 us)
Async XLA Ops:
  17.7 57.4 %all-to-all-start = ((bf16[32,256,128]{2,1,0:T(8,128)(2,1)}), bf16[32,256,128]{2,1,0:T(8,128)(2,1)S(1)}, u32[]{:S(2)}, u32[]{:S(2)}) async-start(bf16[32,256,128]{2,1,0:T(8,128)(2,1)} %rhs_back.1), calls=%async_computation | async-start | bytes 4194304 | tf_op jit(solution)/shard_map/all_to_all | solution.py:385
  75.0 1.3 copy-start.1
  76.4 19.9 %copy-start.3 = (f32[32]{0:T(128)S(1)}, f32[32]{0:T(128)}, u32[]{:S(2)}) copy-start(f32[32]{0:T(128)} %param.9) | copy-start | bytes 388
  93.0 53.3 %all-to-all-start.1 = ((bf16[32,256,128]{2,1,0:T(8,128)(2,1)}), bf16[32,256,128]{2,1,0:T(8,128)(2,1)S(1)}, u32[]{:S(2)}, u32[]{:S(2)}) async-start(bf16[32,256,128]{2,1,0:T(8,128)(2,1)} %get-tuple-element.20), calls=%async_computation.1 | async-start | bytes 4194304 | tf_op jit(solution)/shard_map/all_to_all | solution.py:385
  146.3 1.3 copy-start.2
  178.1 54.8 %all-to-all-start.2 = ((bf16[32,264,128]{2,1,0:T(8,128)(2,1)}), bf16[32,264,128]{2,1,0:T(8,128)(2,1)S(1)}, u32[]{:S(2)}, u32[]{:S(2)}) async-start(bf16[32,264,128]{2,1,0:T(8,128)(2,1)} %normal.2), calls=%async_computation.2 | async-start | bytes 4325376 | tf_op jit(solution)/shard_map/all_to_all | solution.py:385
  232.8 1.4 copy-start

commit v2 on v1

v2 whole, which is shorter than its diff:
```python
import math

import jax
import jax.numpy as jnp
import numpy as np
from jax import lax
from jax.experimental import pallas as pl
from jax.experimental.pallas import tpu as pltpu
from jax.sharding import PartitionSpec as P

K = 1024
F = 2048
ITERS = 2
AXES = ("row", "col")
BF16 = jnp.bfloat16
F32 = jnp.float32
NT = (((1,), (1,)), ((), ()))
VMEM_BYTES = 28 * 2**20


def dot_nn(a, b):
    return jnp.dot(a, b, preferred_element_type=F32)


def dot_nt(a, b):
    return lax.dot_general(a, b, NT, preferred_element_type=F32)


def build_table(taps, bins):
    tap_index = jnp.arange(taps, dtype=jnp.int32)[:, None]
    bin_index = jnp.arange(bins, dtype=jnp.int32)[None, :]
    phase = (tap_index * bin_index % bins).astype(jnp.float32) * (2.0 * math.pi / bins)
    return jnp.stack([jnp.cos(phase), -jnp.sin(phase)], axis=1) / math.sqrt(bins)


def plain_body(transfer, target, zone_mask, dark_weight, reg_weight, momentum):
    dft_table = build_table(K, F)
    mic_gains = jnp.where(zone_mask == 1, jnp.float32(1.0), dark_weight[:, None])
    weight_real = transfer[:, 0]
    weight_imag = transfer[:, 1]
    reg_term = reg_weight[:, None, None]

    def to_taps(spectrum):
        regrouped = lax.all_to_all(spectrum, AXES, split_axis=3, concat_axis=0, tiled=True)
        return jnp.einsum("fctl,kcf->tlk", regrouped, dft_table, precision=lax.Precision.HIGHEST)

    def contract(spec, first, second):
        return jnp.einsum(spec, first, second, preferred_element_type=jnp.float32)

    def back_project(err_real, err_imag):
        spec = "fml,ftm->ftl"
        back_real = contract(spec, weight_real, err_real) + contract(spec, weight_imag, err_imag)
        back_imag = contract(spec, weight_real, err_imag) - contract(spec, weight_imag, err_real)
        return back_real, back_imag

    rhs_error = jnp.where(zone_mask[None, None] == 1, target, jnp.zeros_like(target))
    rhs = to_taps(jnp.stack(back_project(rhs_error[:, 0], rhs_error[:, 1]), axis=1))
    filters = jnp.zeros_like(rhs)
    residual = rhs
    direction = rhs
    for iteration in range(ITERS):
        along_term = jnp.sum(residual * direction)
        to_spectrum = jnp.einsum(
            "tlk,kcf->fctl", direction, dft_table, precision=lax.Precision.HIGHEST
        ).astype(jnp.bfloat16)
        spec = lax.all_to_all(to_spectrum, AXES, split_axis=0, concat_axis=3, tiled=True)
        spec_real = spec[:, 0]
        spec_imag = spec[:, 1]
        form = "fml,ftl->ftm"
        press_real = contract(form, weight_real, spec_real) - contract(form, weight_imag, spec_imag)
        press_imag = contract(form, weight_real, spec_imag) + contract(form, weight_imag, spec_real)
        back_real, back_imag = back_project(
            (mic_gains * press_real).astype(jnp.bfloat16),
            (mic_gains * press_imag).astype(jnp.bfloat16),
        )
        image_taps = to_taps(
            jnp.stack(
                [
                    back_real + reg_term * spec_real.astype(jnp.float32),
                    back_imag + reg_term * spec_imag.astype(jnp.float32),
                ],
                axis=1,
            )
        )
        along_sum, bend_sum = lax.psum((along_term, jnp.sum(direction * image_taps)), AXES)
        step_size = along_sum / bend_sum
        filters = filters + step_size * direction
        residual = residual - step_size * image_taps
        if iteration + 1 < ITERS:
            direction = residual + momentum[iteration] * direction
    return (filters, residual)


def table_factors(devices, bins, taps):
    local = bins // devices
    tap = np.arange(taps)
    scale = 2.0 * math.pi / bins
    coarse = (np.arange(devices // 2)[:, None] * local * tap[None, :]) % bins * scale
    fine = (np.arange(local)[:, None] * tap[None, :]) % bins * scale
    norm = 1.0 / math.sqrt(bins)
    factors = (np.cos(coarse) * norm, np.sin(coarse) * norm, np.cos(fine), np.sin(fine))
    return jnp.asarray(np.concatenate(factors).astype(np.float32))


def table_rows(d, bins, factors, high_ref, low_ref):
    half = factors.shape[0] // 2 - bins
    cos_c = factors[pl.ds(d, 1), :]
    sin_c = factors[pl.ds(half + d, 1), :]
    cos_f = factors[2 * half : 2 * half + bins, :]
    sin_f = factors[2 * half + bins :, :]
    odd = lax.broadcasted_iota(jnp.int32, cos_f.shape, 1) % 2
    sign = (1 - 2 * odd).astype(BF16)
    parts = (cos_c * cos_f - sin_c * sin_f, -(sin_c * cos_f + cos_c * sin_f))
    for c, value in enumerate(parts):
        high = value.astype(BF16)
        low = (value - high.astype(F32)).astype(BF16)
        here = pl.ds((2 * d + c) * bins, bins)
        there = pl.ds((2 * (d + half) + c) * bins, bins)
        high_ref[here, :] = high
        low_ref[here, :] = low
        high_ref[there, :] = high * sign
        low_ref[there, :] = low * sign


LANES = 128
PAD = 8


def turn_out(turn_ref, out_ref, targets):
    devices, _, width = out_ref.shape
    pitch = width + PAD
    step_rows = targets * pitch
    blocks = turn_ref.shape[0] // step_rows
    each = devices // blocks

    def step(pair, carry):
        for block in range(blocks):
            halves = []
            for side in range(2):
                start = block * step_rows + (2 * pair + side) * pitch
                halves.append(turn_ref[pl.ds(start, width), :].T.reshape(each, 8, width))
            both = jnp.concatenate(halves, axis=1).astype(BF16)
            out_ref[block * each : (block + 1) * each, pl.ds(16 * pair, 16), :] = both
        return carry

    lax.fori_loop(0, targets // 2, step, 0)


def turn_in(in_ref, turn_ref, targets):
    devices, _, width = in_ref.shape
    pitch = width + PAD
    step_rows = targets * pitch
    blocks = turn_ref.shape[0] // step_rows
    each = devices // blocks

    def step(pair, carry):
        for block in range(blocks):
            part = in_ref[block * each : (block + 1) * each, pl.ds(16 * pair, 16), :].astype(F32)
            for side in range(2):
                half = part[:, 8 * side : 8 * side + 8, :].reshape(LANES, width)
                start = block * step_rows + (2 * pair + side) * pitch
                turn_ref[pl.ds(start, width), :] = half.T
        return carry

    lax.fori_loop(0, targets // 2, step, 0)


def load_bin(turn_ref, row, targets, width):
    stride = width + PAD
    step_rows = targets * stride
    return jnp.concatenate(
        [
            turn_ref[pl.ds(block * step_rows + row, targets, stride=stride), :]
            for block in range(turn_ref.shape[0] // step_rows)
        ],
        axis=1,
    )


def store_bin(turn_ref, row, targets, width, values):
    stride = width + PAD
    step_rows = targets * stride
    for block in range(turn_ref.shape[0] // step_rows):
        part = values[:, block * LANES : (block + 1) * LANES]
        turn_ref[pl.ds(block * step_rows + row, targets, stride=stride), :] = part


def store_sums(out_ref, along, bend):
    row = lax.broadcasted_iota(jnp.int32, along.shape, 0)
    value = jnp.where(row < 3, along, bend)
    first = value.astype(BF16).astype(F32)
    second = (value - first).astype(BF16).astype(F32)
    third = value - first - second
    term = jnp.where(row % 3 == 0, first, jnp.where(row % 3 == 1, second, third))
    term = jnp.where(row < 6, term, 0.0).astype(BF16)
    rows = out_ref.shape[1]
    out_ref[:, rows - 8 : rows, :] = jnp.broadcast_to(term[None], (out_ref.shape[0],) + term.shape)


def step_of(back_ref):
    rows = back_ref.shape[1]
    sums = jnp.sum(back_ref[:, rows - 8 : rows, :].astype(F32), axis=0)
    along = sums[0:1, 0:1] + sums[1:2, 0:1] + sums[2:3, 0:1]
    bend = sums[3:4, 0:1] + sums[4:5, 0:1] + sums[5:6, 0:1]
    return along / bend


def back_of(err, weight, half):
    turned = jnp.concatenate([err[half:], -err[:half]], axis=0)
    return dot_nn(err, weight[0]) + dot_nn(turned, weight[1])


GROUP = 8
SLOTS = 3


def group_copies(arrays, buffers, sems, g):
    slot = g % SLOTS
    return [
        pltpu.make_async_copy(array.at[pl.ds(g * GROUP, GROUP)], buffer.at[slot], sems.at[n, slot])
        for n, (array, buffer) in enumerate(zip(arrays, buffers))
    ]


def over_bins(arrays, buffers, sems, one_bin, one_group=None):
    groups = arrays[0].shape[0] // GROUP
    for g in range(min(SLOTS, groups)):
        for copy in group_copies(arrays, buffers, sems, g):
            copy.start()

    def group(g, carry):
        for copy in group_copies(arrays, buffers, sems, g):
            copy.wait()
        for b in range(GROUP):
            slices = [buffer.at[g % SLOTS, b] for buffer in buffers]
            carry = one_bin(g * GROUP + b, *slices, carry)
        if one_group is not None:
            one_group(g, groups)

        @pl.when(g + SLOTS < groups)
        def _():
            for copy in group_copies(arrays, buffers, sems, g + SLOTS):
                copy.start()

        return carry

    return lambda carry: lax.fori_loop(0, groups, group, carry)


def rhs_kernel(
    bright_ref, gains_ref, momentum_ref, factors, w_hbm, target_hbm,
    out_ref, high_ref, low_ref, w_buf, target_buf, back_buf, sems,
):
    bins, _, targets, mics = target_hbm.shape
    bright = jnp.concatenate([bright_ref[...], bright_ref[...]], axis=0) == 1.0

    def one_bin(j, weight, target, carry):
        wanted = target[...].reshape(2 * targets, mics).astype(F32)
        err = jnp.where(bright, wanted, 0.0).astype(BF16)
        back = back_of(err, weight, targets)
        store_bin(back_buf, j, targets, 2 * bins, back[:targets])
        store_bin(back_buf, bins + j, targets, 2 * bins, back[targets:])
        return carry

    def one_group(g, groups):
        each = (factors.shape[0] // 2 - bins) // groups
        for d in range(each):
            table_rows(g * each + d, bins, factors, high_ref, low_ref)

    over_bins((w_hbm, target_hbm), (w_buf, target_buf), sems, one_bin, one_group)(0)
    turn_out(back_buf, out_ref, targets)


def normal_kernel(
    spec_ref, gains_ref, reg_ref, along_ref, w_hbm, out_ref, w_buf, spec_buf, back_buf, sems
):
    bins = w_hbm.shape[0]
    targets = gains_ref.shape[0]

    def one_bin(j, weight, bend):
        real = load_bin(spec_buf, j, targets, 2 * bins)
        imag = load_bin(spec_buf, bins + j, targets, 2 * bins)
        wide = jnp.concatenate([real, imag], axis=0)
        spec = wide.astype(BF16)
        turned = jnp.concatenate([-imag, real], axis=0).astype(BF16)
        press = dot_nt(spec, weight[0]) + dot_nt(turned, weight[1])
        back = back_of((gains * press).astype(BF16), weight, targets)
        back = back + reg_ref[j] * wide
        store_bin(back_buf, j, targets, 2 * bins, back[:targets])
        store_bin(back_buf, bins + j, targets, 2 * bins, back[targets:])
        return bend + wide * back

    run = over_bins((w_hbm,), (w_buf,), sems, one_bin)
    gains = jnp.concatenate([gains_ref[...], gains_ref[...]], axis=0)
    turn_in(spec_ref, spec_buf, targets)
    bend = run(jnp.zeros((2 * targets, w_hbm.shape[3]), F32))
    turn_out(back_buf, out_ref, targets)
    store_sums(out_ref, along_ref[...], jnp.sum(bend))


PIECES = 4


def taps_of(back_ref, high_ref, low_ref, count):
    rows = high_ref.shape[0] // PIECES
    per = back_ref.shape[0] // PIECES
    total = None
    for c in range(PIECES):
        part = pl.ds(c * rows, rows)
        block = jnp.concatenate([back_ref[c * per + d, :count, :] for d in range(per)], axis=1)
        term = dot_nn(block, high_ref[part, :]) + dot_nn(block, low_ref[part, :])
        total = term if total is None else total + term
    return total


def spectrum_to(out_ref, direction, high_ref, low_ref):
    rows = high_ref.shape[0] // PIECES
    per = out_ref.shape[0] // PIECES
    width = out_ref.shape[2]
    count = direction.shape[0]
    high = direction.astype(BF16)
    low = (direction - high.astype(F32)).astype(BF16)
    both = jnp.concatenate([high, low], axis=0)
    for c in range(PIECES):
        part = pl.ds(c * rows, rows)
        wide = dot_nt(both, high_ref[part, :])
        spec = wide[:count] + wide[count:] + dot_nt(high, low_ref[part, :])
        for d in range(per):
            out_ref[c * per + d] = spec[:, d * width : (d + 1) * width].astype(BF16)


def first_kernel(back_ref, high_ref, low_ref, rhs_ref, spec_ref, along_ref):
    rhs = taps_of(back_ref, high_ref, low_ref, rhs_ref.shape[0])
    rhs_ref[...] = rhs
    along_ref[...] = jnp.broadcast_to(jnp.sum(rhs * rhs), along_ref.shape)
    spectrum_to(spec_ref, rhs, high_ref, low_ref)


def middle_kernel(
    back_ref, rhs_ref, momentum_ref, high_ref, low_ref, residual_ref, spec_ref, along_ref, step_ref
):
    step = step_of(back_ref)
    step_ref[...] = jnp.broadcast_to(step, step_ref.shape)
    image = taps_of(back_ref, high_ref, low_ref, residual_ref.shape[0])
    rhs = rhs_ref[...]
    residual = rhs - step * image
    direction = residual + momentum_ref[0:1, 0:1] * rhs
    residual_ref[...] = residual
    along_ref[...] = jnp.broadcast_to(jnp.sum(residual * direction), along_ref.shape)
    spectrum_to(spec_ref, direction, high_ref, low_ref)


def last_kernel(
    back_ref, rhs_ref, residual_ref, step_ref, momentum_ref, high_ref, low_ref,
    filters_out, residual_out,
):
    step = step_of(back_ref)
    rhs = rhs_ref[...]
    residual = residual_ref[...]
    direction = residual + momentum_ref[0:1, 0:1] * rhs
    filters_out[...] = step_ref[0:1, 0:1] * rhs + step * direction
    image = taps_of(back_ref, high_ref, low_ref, residual_ref.shape[0])
    residual_out[...] = residual - step * image


def vmem():
    return pl.BlockSpec(memory_space=pltpu.VMEM)


def smem():
    return pl.BlockSpec(memory_space=pltpu.SMEM)


def hbm():
    return pl.BlockSpec(memory_space=pltpu.HBM)


def kernel_body(transfer, target, zone_mask, dark_weight, reg_weight, momentum):
    bins, _, mics, speakers = transfer.shape
    targets = target.shape[2]
    devices = F // bins
    rows = targets * (speakers // devices)
    block = pltpu.VMEM((devices, rows, 2 * bins), BF16)
    summed = pltpu.VMEM((devices, rows + 8, 2 * bins), BF16)
    tile = jax.ShapeDtypeStruct((8, 128), F32)
    taps = jax.ShapeDtypeStruct((rows, K), F32)
    gains = jnp.where(zone_mask == 1, jnp.float32(1.0), dark_weight[:, None])
    bright = (zone_mask == 1).astype(F32)
    factors = pltpu.with_memory_space_constraint(table_factors(devices, F, K), pltpu.HBM)
    target = pltpu.with_memory_space_constraint(target, pltpu.HBM)
    momentum = jnp.broadcast_to(momentum, (8, 128))
    weights = pltpu.VMEM((SLOTS, GROUP) + transfer.shape[1:], BF16)
    turning = pltpu.VMEM((speakers // LANES * targets * (2 * bins + PAD), LANES), F32)
    sems = pltpu.SemaphoreType.DMA((2, SLOTS))

    def exchange(payload):
        received = lax.all_to_all(payload, AXES, split_axis=0, concat_axis=0, tiled=True)
        return pltpu.with_memory_space_constraint(received, pltpu.VMEM)

    def call(kernel, name, in_specs, out_shape, scratch=()):
        return pl.pallas_call(
            kernel,
            in_specs=in_specs,
            out_specs=jax.tree.map(lambda _: vmem(), out_shape),
            out_shape=out_shape,
            scratch_shapes=scratch,
            compiler_params=pltpu.CompilerParams(vmem_limit_bytes=VMEM_BYTES),
            name=name,
        )

    normal = call(
        normal_kernel, "normal", [vmem(), vmem(), smem(), vmem(), hbm()],
        summed, [weights, turning, turning, sems],
    )
    table = pltpu.VMEM((2 * F, K), BF16)
    wanted = pltpu.VMEM((SLOTS, GROUP) + target.shape[1:], BF16)
    back, high, low = call(
        rhs_kernel, "rhs_back", [vmem()] * 4 + [hbm(), hbm()], [block, table, table],
        [weights, wanted, turning, sems],
    )(bright, gains, momentum, factors, transfer, target)
    high = pltpu.with_memory_space_constraint(high, pltpu.VMEM)
    low = pltpu.with_memory_space_constraint(low, pltpu.VMEM)
    rhs, spec, along = call(first_kernel, "first_taps", [vmem()] * 3, [taps, block, tile])(
        exchange(back), high, low
    )
    back = normal(exchange(spec), gains, reg_weight, along, transfer)
    residual, spec, along, step = call(
        middle_kernel, "middle_taps", [vmem()] * 5, [taps, block, tile, tile],
    )(exchange(back), rhs, momentum, high, low)
    back = normal(exchange(spec), gains, reg_weight, along, transfer)
    filters, residual = call(
        last_kernel, "last_taps", [vmem()] * 7, [taps, taps]
    )(exchange(back), rhs, residual, step, momentum, high, low)
    shape = (targets, speakers // devices, K)
    return filters.reshape(shape), residual.reshape(shape)


def body(transfer, target, *rest):
    bins, _, mics, speakers = transfer.shape
    devices = F // bins
    whole_tiles = (
        bins == 64
        and speakers == 8 * devices
        and speakers % 128 == 0
        and mics % 128 == 0
        and target.shape[2] == 32
        and devices % 4 == 0
    )
    return (kernel_body if whole_tiles else plain_body)(transfer, target, *rest)


def solution(mesh):
    in_specs = (
        P(AXES, None, None, None),
        P(AXES, None, None, None),
        P(),
        P(),
        P(AXES),
        P(),
    )
    out_specs = (P(None, AXES, None), P(None, AXES, None))
    return jax.shard_map(body, mesh=mesh, in_specs=in_specs, out_specs=out_specs, check_vma=False)
```

time: 402 us -> 365 us (0.908)
  blocking collectives: 109 us -> 269 us
  waiting for transfers between devices: 136 us -> 0 us
  Pallas kernels: 123 us -> 93.8 us
  starting transfers between devices: 13.8 us -> 0 us
  other arithmetic: 14.7 us -> 0.94 us
  local copies, waits for them, and re-layouts: 4.69 us -> 0.02 us
    all_to_all x2 -> x5, blocking collectives: 109 us -> 269 us  [exchange(): lax.all_to_all(payload, AXES, split_axis=0, concat_axis=0, tiled=True)]
    all_to_all x3 -> x0, waiting for transfers between devices: 136 us -> none  [exchange(): lax.all_to_all(payload, AXES, split_axis=0, concat_axis=0, tiled=True)]
    pallas_call x6, Pallas kernels: 123 us -> 93.8 us  [the longest x2 48.9 us: kernel_body(): back = normal(exchange(spec), gains, reg_weight, along, transfer)]
    all_to_all x3 -> x0, starting transfers between devices: 13.8 us -> none  [exchange(): lax.all_to_all(payload, AXES, split_axis=0, concat_axis=0, tiled=True)]
    convert_element_type x1, other arithmetic: 8.19 us -> 0.01 us  [kernel_body(): bright = (zone_mask == 1).astype(F32)]
  transfers between devices with their start and end apart: 3 -> 0, of which waited for: 3 -> 0; matrix products, arithmetic and copies ran while one was open for 4% -> 0% of each run, Pallas kernels for 0% -> 0%
where the time goes in v2:
time: 365 us
  blocking collectives  269 us (74%)
  Pallas kernels  93.8 us (26%)
    all_to_all x5, blocking collectives, exchange(): lax.all_to_all(payload, AXES, split_axis=0, concat_axis=0, tiled=True)  269 us
    pallas_call x2, Pallas kernels, kernel_body(): back = normal(exchange(spec), gains, reg_weight, along, transfer)  48.9 us
    pallas_call x1, Pallas kernels, kernel_body(): call(rhs_kernel, 'rhs_back', [vmem()] * 4 + [hbm(), hbm()], [block, table...  16.4 us
    pallas_call x1, Pallas kernels, kernel_body(): call(middle_kernel, 'middle_taps', [vmem()] * 5, [taps, block, tile, tile])  11.4 us
    pallas_call x1, Pallas kernels, kernel_body(): call(first_kernel, 'first_taps', [vmem()] * 3, [taps, block, tile])  11.2 us

profile of v2, /device:TPU:0, one launch (start us, length us, event | category | flops | bytes accessed | tf_op | source)
XLA Modules:
  0.0 364.8 jit_solution(10421872962088168048)
XLA Ops:
  1.3 0.9 broadcast_select_fusion
  2.2 16.4 %rhs_back.1 = (bf16[32,256,128]{2,1,0:T(8,128)(2,1)S(1)}, bf16[4096,1024]{1,0:T(8,128)(2,1)S(1)}, bf16[4096,1024]{1,0:T(8,128)(2,1)S(1)}) custom-call(f32[32,512]{1,0:T(8,128)S(1)} %convert_element_type.3.bright_ref, f32[32,512]{1,0:T(8,128)S(1)} %get-tuple-element.26.gains_ref, f32[8,128]{1,0:T(8,128)S(1)} %broadcast_in_dim.20.momentum_ref, ...), custom_call_target="tpu_custom_call" | custom-call | tf_op jit(solution)/shard_map/rhs_back/pallas_call | solution.py:417
  18.6 0.0 copy-start
  18.6 57.2 %all_to_all.25.back_ref = bf16[32,256,128]{2,1,0:T(8,128)(2,1)S(1)} all-to-all(bf16[32,256,128]{2,1,0:T(8,128)(2,1)S(1)} %get-tuple-element.14), channel_id=1, replica_groups=mesh['row'=4,'col'=8] {'row','col'}, dimensions={0} | all-to-all | bytes 4194304 | tf_op jit(solution)/shard_map/all_to_all | solution.py:397
  75.8 11.2 %first_taps.1 = (f32[256,1024]{1,0:T(8,128)S(1)}, bf16[32,256,128]{2,1,0:T(8,128)(2,1)S(1)}, f32[8,128]{1,0:T(8,128)S(1)}) custom-call(bf16[32,256,128]{2,1,0:T(8,128)(2,1)S(1)} %all_to_all.25.back_ref, bf16[4096,1024]{1,0:T(8,128)(2,1)S(1)} %get-tuple-element.15.high_ref, bf16[4096,1024]{1,0:T(8,128)(2,1)S(1)} %get-tuple-element.16.low_ref), custom_call_target="tpu_custom_call" | custom-call | tf_op jit(solution)/shard_map/first_taps/pallas_call | solution.py:423
  87.0 0.0 copy-done
  87.0 0.0 copy-start.1
  87.0 52.1 %all_to_all.26.spec_ref = bf16[32,256,128]{2,1,0:T(8,128)(2,1)S(1)} all-to-all(bf16[32,256,128]{2,1,0:T(8,128)(2,1)S(1)} %get-tuple-element.17), channel_id=1, replica_groups=mesh['row'=4,'col'=8] {'row','col'}, dimensions={0} | all-to-all | bytes 4194304 | tf_op jit(solution)/shard_map/all_to_all | solution.py:397
  139.2 0.0 slice-start
  139.2 0.0 copy-done.1
  139.2 0.0 slice-start.1
  139.2 24.6 %normal.2 = bf16[32,264,128]{2,1,0:T(8,128)(2,1)S(1)} custom-call(bf16[32,256,128]{2,1,0:T(8,128)(2,1)S(1)} %all_to_all.26.spec_ref, f32[32,512]{1,0:T(8,128)S(1)} %get-tuple-element.26.gains_ref, f32[64]{0:T(128)S(1)} %copy-done.1, f32[8,128]{1,0:T(8,128)S(1)} %get-tuple-element.18.along_ref, bf16[64,2,512,256]{3,2,1,0:T(8,128)(2,1)} %w_hbm.5), custom_call_target="tpu_custom_call" | custom-call | tf_op jit(solution)/shard_map/normal/pallas_call | solution.py:426
  163.7 53.7 %all_to_all.27.back_ref = bf16[32,264,128]{2,1,0:T(8,128)(2,1)S(1)} all-to-all(bf16[32,264,128]{2,1,0:T(8,128)(2,1)S(1)} %normal.2), channel_id=1, replica_groups=mesh['row'=4,'col'=8] {'row','col'}, dimensions={0} | all-to-all | bytes 4325376 | tf_op jit(solution)/shard_map/all_to_all | solution.py:397
  217.5 0.0 slice-done
  217.5 0.0 slice-done.1
  217.5 11.4 %middle_taps.1 = (f32[256,1024]{1,0:T(8,128)S(1)}, bf16[32,256,128]{2,1,0:T(8,128)(2,1)S(1)}, f32[8,128]{1,0:T(8,128)S(1)}, f32[8,128]{1,0:T(8,128)S(1)}) custom-call(bf16[32,264,128]{2,1,0:T(8,128)(2,1)S(1)} %all_to_all.27.back_ref, f32[256,1024]{1,0:T(8,128)S(1)} %get-tuple-element.19.rhs_ref, f32[8,128]{1,0:T(8,128)S(1)} %broadcast_in_dim.20.momentum_ref, ...), custom_call_target="tpu_custom_call" | custom-call | tf_op jit(solution)/shard_map/middle_taps/pallas_call | solution.py:427
  228.9 52.0 %all_to_all.28.spec_ref = bf16[32,256,128]{2,1,0:T(8,128)(2,1)S(1)} all-to-all(bf16[32,256,128]{2,1,0:T(8,128)(2,1)S(1)} %get-tuple-element.20), channel_id=1, replica_groups=mesh['row'=4,'col'=8] {'row','col'}, dimensions={0} | all-to-all | bytes 4194304 | tf_op jit(solution)/shard_map/all_to_all | solution.py:397
  280.9 24.3 %normal.3 = bf16[32,264,128]{2,1,0:T(8,128)(2,1)S(1)} custom-call(bf16[32,256,128]{2,1,0:T(8,128)(2,1)S(1)} %all_to_all.28.spec_ref, f32[32,512]{1,0:T(8,128)S(1)} %get-tuple-element.26.gains_ref, f32[64]{0:T(128)S(1)} %copy-done.1, f32[8,128]{1,0:T(8,128)S(1)} %get-tuple-element.21.along_ref, bf16[64,2,512,256]{3,2,1,0:T(8,128)(2,1)} %w_hbm.5), custom_call_target="tpu_custom_call" | custom-call | tf_op jit(solution)/shard_map/normal/pallas_call | solution.py:430
  305.2 53.7 %all_to_all.29.back_ref = bf16[32,264,128]{2,1,0:T(8,128)(2,1)S(1)} all-to-all(bf16[32,264,128]{2,1,0:T(8,128)(2,1)S(1)} %normal.3), channel_id=1, replica_groups=mesh['row'=4,'col'=8] {'row','col'}, dimensions={0} | all-to-all | bytes 4325376 | tf_op jit(solution)/shard_map/all_to_all | solution.py:397
  358.9 5.9 %last_taps.1 = (f32[256,1024]{1,0:T(8,128)}, f32[256,1024]{1,0:T(8,128)}) custom-call(bf16[32,264,128]{2,1,0:T(8,128)(2,1)S(1)} %all_to_all.29.back_ref, f32[256,1024]{1,0:T(8,128)S(1)} %get-tuple-element.19.rhs_ref, f32[256,1024]{1,0:T(8,128)S(1)} %get-tuple-element.22.residual_ref, f32[8,128]{1,0:T(8,128)S(1)} %get-tuple-element.23.step_ref, ...), custom_call_target="tpu_custom_call" | custom-call | tf_op jit(solution)/shard_map/last_taps/pallas_call | solution.py:431
  (3 shorter events, 0.0 us)
Async XLA Ops:
  18.6 68.4 %copy-start = (bf16[4096,1024]{1,0:T(8,128)(2,1)}, bf16[4096,1024]{1,0:T(8,128)(2,1)S(1)}, u32[]{:S(2)}) copy-start(bf16[4096,1024]{1,0:T(8,128)(2,1)S(1)} %get-tuple-element.16.low_ref) | copy-start | bytes 25165828
  87.0 52.2 %copy-start.1 = (f32[64]{0:T(128)S(1)}, f32[64]{0:T(128)}, u32[]{:S(2)}) copy-start(f32[64]{0:T(128)} %reg_ref.3) | copy-start | bytes 772
  139.2 78.3 %slice-start = ((s8[8388608]{0:T(1024)(128)(4,1)}), s8[4194304]{0:T(1024)(128)(4,1)S(1)}, s32[]{:S(2)}) async-start(s8[8388608]{0:T(1024)(128)(4,1)} %bitcast.4), calls=%async_computation.5 | async-start | bytes 8388608
  139.2 78.3 %slice-start.1 = ((s8[8388608]{0:T(1024)(128)(4,1)}), s8[4194304]{0:T(1024)(128)(4,1)S(1)}, s32[]{:S(2)}) async-start(s8[8388608]{0:T(1024)(128)(4,1)} %bitcast.4), calls=%async_computation.6 | async-start | bytes 8388608

commit v3 on v2

--- a/solution.py
+++ b/solution.py
@@ -212,6 +212,7 @@
 
 GROUP = 8
 SLOTS = 3
+AHEAD = 2
 
 
 def group_copies(arrays, buffers, sems, g):
@@ -222,7 +223,7 @@
     ]
 
 
-def over_bins(arrays, buffers, sems, one_bin, one_group=None):
+def over_bins(arrays, buffers, sems, prepare, one_bin, one_group=None):
     groups = arrays[0].shape[0] // GROUP
     for g in range(min(SLOTS, groups)):
         for copy in group_copies(arrays, buffers, sems, g):
@@ -231,11 +232,14 @@
     def group(g, carry):
         for copy in group_copies(arrays, buffers, sems, g):
             copy.wait()
+        slices = [[buffer.at[g % SLOTS, b] for buffer in buffers] for b in range(GROUP)]
+        begun = [prepare(g * GROUP + b, *slices[b]) for b in range(AHEAD)]
         for b in range(GROUP):
-            slices = [buffer.at[g % SLOTS, b] for buffer in buffers]
-            carry = one_bin(g * GROUP + b, *slices, carry)
+            if b + AHEAD < GROUP:
+                begun.append(prepare(g * GROUP + b + AHEAD, *slices[b + AHEAD]))
+            carry = one_bin(g * GROUP + b, *slices[b], begun[b], carry)
         if one_group is not None:
-            one_group(g, groups)
+            one_group(g)
 
         @pl.when(g + SLOTS < groups)
         def _():
@@ -252,22 +256,30 @@
     out_ref, high_ref, low_ref, w_buf, target_buf, back_buf, sems,
 ):
     bins, _, targets, mics = target_hbm.shape
-    bright = jnp.concatenate([bright_ref[...], bright_ref[...]], axis=0) == 1.0
-
-    def one_bin(j, weight, target, carry):
-        wanted = target[...].reshape(2 * targets, mics).astype(F32)
-        err = jnp.where(bright, wanted, 0.0).astype(BF16)
+    bright = jnp.concatenate([bright_ref[...], bright_ref[...]], axis=0).astype(BF16)
+
+    def prepare(j, weight, target):
+        return target[...].reshape(2 * targets, mics) * bright
+
+    def one_bin(j, weight, target, err, carry):
         back = back_of(err, weight, targets)
         store_bin(back_buf, j, targets, 2 * bins, back[:targets])
         store_bin(back_buf, bins + j, targets, 2 * bins, back[targets:])
         return carry
 
-    def one_group(g, groups):
-        each = (factors.shape[0] // 2 - bins) // groups
+    half = factors.shape[0] // 2 - bins
+    groups = bins // GROUP
+    first = half // 2
+    each = (half - first) // groups
+
+    def one_group(g):
         for d in range(each):
-            table_rows(g * each + d, bins, factors, high_ref, low_ref)
-
-    over_bins((w_hbm, target_hbm), (w_buf, target_buf), sems, one_bin, one_group)(0)
+            table_rows(first + g * each + d, bins, factors, high_ref, low_ref)
+
+    run = over_bins((w_hbm, target_hbm), (w_buf, target_buf), sems, prepare, one_bin, one_group)
+    for d in range(first):
+        table_rows(d, bins, factors, high_ref, low_ref)
+    run(0)
     turn_out(back_buf, out_ref, targets)
 
 
@@ -277,20 +289,24 @@
     bins = w_hbm.shape[0]
     targets = gains_ref.shape[0]
 
-    def one_bin(j, weight, bend):
+    def prepare(j, weight):
         real = load_bin(spec_buf, j, targets, 2 * bins)
         imag = load_bin(spec_buf, bins + j, targets, 2 * bins)
         wide = jnp.concatenate([real, imag], axis=0)
         spec = wide.astype(BF16)
         turned = jnp.concatenate([-imag, real], axis=0).astype(BF16)
         press = dot_nt(spec, weight[0]) + dot_nt(turned, weight[1])
-        back = back_of((gains * press).astype(BF16), weight, targets)
+        return wide, (gains * press).astype(BF16)
+
+    def one_bin(j, weight, prepared, bend):
+        wide, err = prepared
+        back = back_of(err, weight, targets)
         back = back + reg_ref[j] * wide
         store_bin(back_buf, j, targets, 2 * bins, back[:targets])
         store_bin(back_buf, bins + j, targets, 2 * bins, back[targets:])
         return bend + wide * back
 
-    run = over_bins((w_hbm,), (w_buf,), sems, one_bin)
+    run = over_bins((w_hbm,), (w_buf,), sems, prepare, one_bin)
     gains = jnp.concatenate([gains_ref[...], gains_ref[...]], axis=0)
     turn_in(spec_ref, spec_buf, targets)
     bend = run(jnp.zeros((2 * targets, w_hbm.shape[3]), F32))
@@ -313,20 +329,42 @@
     return total
 
 
+def mirror_matrix(bins):
+    row = lax.broadcasted_iota(jnp.int32, (4 * bins, 2 * bins), 0)
+    col = lax.broadcasted_iota(jnp.int32, (4 * bins, 2 * bins), 1)
+    part = col // bins
+    place = col % bins
+    source = jnp.where(place == 0, (2 + part) * bins, part * bins + bins - place)
+    sign = (1 - 2 * part).astype(F32)
+    return jnp.where(row == source, sign, 0.0).astype(BF16)
+
+
 def spectrum_to(out_ref, direction, high_ref, low_ref):
-    rows = high_ref.shape[0] // PIECES
-    per = out_ref.shape[0] // PIECES
-    width = out_ref.shape[2]
+    devices, _, width = out_ref.shape
+    half = devices // 2
+    per = half // (PIECES // 2)
     count = direction.shape[0]
     high = direction.astype(BF16)
     low = (direction - high.astype(F32)).astype(BF16)
     both = jnp.concatenate([high, low], axis=0)
-    for c in range(PIECES):
-        part = pl.ds(c * rows, rows)
+    mirror = mirror_matrix(width // 2)
+
+    def blocks(first, number):
+        part = pl.ds(first * width, number * width)
         wide = dot_nt(both, high_ref[part, :])
         spec = wide[:count] + wide[count:] + dot_nt(high, low_ref[part, :])
+        return spec.astype(BF16)
+
+    after = blocks(half, 1)
+    for c in reversed(range(half // per)):
+        spec = blocks(c * per, per)
+        wider = jnp.concatenate([spec, after], axis=1)
         for d in range(per):
-            out_ref[c * per + d] = spec[:, d * width : (d + 1) * width].astype(BF16)
+            here = c * per + d
+            out_ref[here] = spec[:, d * width : (d + 1) * width]
+            pair = wider[:, d * width : (d + 2) * width]
+            out_ref[devices - 1 - here] = dot_nn(pair, mirror).astype(BF16)
+        after = spec[:, :width]
 
 
 def first_kernel(back_ref, high_ref, low_ref, rhs_ref, spec_ref, along_ref):

time: 365 us -> 356 us (0.975)
  Pallas kernels: 93.8 us -> 84.6 us
    pallas_call x2, Pallas kernels: 48.9 us -> 43.8 us  [kernel_body(): back = normal(exchange(spec), gains, reg_weight, along, transfer)]
where the time goes in v3:
time: 356 us
  blocking collectives  269 us (76%)
  Pallas kernels  84.6 us (24%)
    all_to_all x5, blocking collectives, exchange(): lax.all_to_all(payload, AXES, split_axis=0, concat_axis=0, tiled=True)  269 us
    pallas_call x2, Pallas kernels, kernel_body(): back = normal(exchange(spec), gains, reg_weight, along, transfer)  43.8 us
    pallas_call x1, Pallas kernels, kernel_body(): call(rhs_kernel, 'rhs_back', [vmem()] * 4 + [hbm(), hbm()], [block, table...  15.8 us
    pallas_call x1, Pallas kernels, kernel_body(): call(middle_kernel, 'middle_taps', [vmem()] * 5, [taps, block, tile, tile])  9.61 us
    pallas_call x1, Pallas kernels, kernel_body(): call(first_kernel, 'first_taps', [vmem()] * 3, [taps, block, tile])  9.43 us

profile of v3, /device:TPU:0, one launch (start us, length us, event | category | flops | bytes accessed | tf_op | source)
XLA Modules:
  0.0 355.6 jit_solution(14973929711459981227)
XLA Ops:
  1.3 0.9 broadcast_select_fusion
  2.2 15.8 %rhs_back.1 = (bf16[32,256,128]{2,1,0:T(8,128)(2,1)S(1)}, bf16[4096,1024]{1,0:T(8,128)(2,1)S(1)}, bf16[4096,1024]{1,0:T(8,128)(2,1)S(1)}) custom-call(f32[32,512]{1,0:T(8,128)S(1)} %convert_element_type.3.bright_ref, f32[32,512]{1,0:T(8,128)S(1)} %get-tuple-element.26.gains_ref, f32[8,128]{1,0:T(8,128)S(1)} %broadcast_in_dim.20.momentum_ref, ...), custom_call_target="tpu_custom_call" | custom-call | tf_op jit(solution)/shard_map/rhs_back/pallas_call | solution.py:455
  18.1 0.0 copy-start
  18.1 57.2 %all_to_all.25.back_ref = bf16[32,256,128]{2,1,0:T(8,128)(2,1)S(1)} all-to-all(bf16[32,256,128]{2,1,0:T(8,128)(2,1)S(1)} %get-tuple-element.14), channel_id=1, replica_groups=mesh['row'=4,'col'=8] {'row','col'}, dimensions={0} | all-to-all | bytes 4194304 | tf_op jit(solution)/shard_map/all_to_all | solution.py:435
  75.3 9.4 %first_taps.1 = (f32[256,1024]{1,0:T(8,128)S(1)}, bf16[32,256,128]{2,1,0:T(8,128)(2,1)S(1)}, f32[8,128]{1,0:T(8,128)S(1)}) custom-call(bf16[32,256,128]{2,1,0:T(8,128)(2,1)S(1)} %all_to_all.25.back_ref, bf16[4096,1024]{1,0:T(8,128)(2,1)S(1)} %get-tuple-element.15.high_ref, bf16[4096,1024]{1,0:T(8,128)(2,1)S(1)} %get-tuple-element.16.low_ref), custom_call_target="tpu_custom_call" | custom-call | tf_op jit(solution)/shard_map/first_taps/pallas_call | solution.py:461
  84.7 0.0 copy-done
  84.7 0.0 copy-start.1
  84.7 52.1 %all_to_all.26.spec_ref = bf16[32,256,128]{2,1,0:T(8,128)(2,1)S(1)} all-to-all(bf16[32,256,128]{2,1,0:T(8,128)(2,1)S(1)} %get-tuple-element.17), channel_id=1, replica_groups=mesh['row'=4,'col'=8] {'row','col'}, dimensions={0} | all-to-all | bytes 4194304 | tf_op jit(solution)/shard_map/all_to_all | solution.py:435
  136.9 0.0 slice-start
  136.9 0.0 copy-done.1
  136.9 0.0 slice-start.1
  136.9 22.0 %normal.2 = bf16[32,264,128]{2,1,0:T(8,128)(2,1)S(1)} custom-call(bf16[32,256,128]{2,1,0:T(8,128)(2,1)S(1)} %all_to_all.26.spec_ref, f32[32,512]{1,0:T(8,128)S(1)} %get-tuple-element.26.gains_ref, f32[64]{0:T(128)S(1)} %copy-done.1, f32[8,128]{1,0:T(8,128)S(1)} %get-tuple-element.18.along_ref, bf16[64,2,512,256]{3,2,1,0:T(8,128)(2,1)} %w_hbm.5), custom_call_target="tpu_custom_call" | custom-call | tf_op jit(solution)/shard_map/normal/pallas_call | solution.py:464
  158.9 53.7 %all_to_all.27.back_ref = bf16[32,264,128]{2,1,0:T(8,128)(2,1)S(1)} all-to-all(bf16[32,264,128]{2,1,0:T(8,128)(2,1)S(1)} %normal.2), channel_id=1, replica_groups=mesh['row'=4,'col'=8] {'row','col'}, dimensions={0} | all-to-all | bytes 4325376 | tf_op jit(solution)/shard_map/all_to_all | solution.py:435
  212.6 0.0 slice-done
  212.6 0.0 slice-done.1
  212.6 9.6 %middle_taps.1 = (f32[256,1024]{1,0:T(8,128)S(1)}, bf16[32,256,128]{2,1,0:T(8,128)(2,1)S(1)}, f32[8,128]{1,0:T(8,128)S(1)}, f32[8,128]{1,0:T(8,128)S(1)}) custom-call(bf16[32,264,128]{2,1,0:T(8,128)(2,1)S(1)} %all_to_all.27.back_ref, f32[256,1024]{1,0:T(8,128)S(1)} %get-tuple-element.19.rhs_ref, f32[8,128]{1,0:T(8,128)S(1)} %broadcast_in_dim.20.momentum_ref, ...), custom_call_target="tpu_custom_call" | custom-call | tf_op jit(solution)/shard_map/middle_taps/pallas_call | solution.py:465
  222.2 52.0 %all_to_all.28.spec_ref = bf16[32,256,128]{2,1,0:T(8,128)(2,1)S(1)} all-to-all(bf16[32,256,128]{2,1,0:T(8,128)(2,1)S(1)} %get-tuple-element.20), channel_id=1, replica_groups=mesh['row'=4,'col'=8] {'row','col'}, dimensions={0} | all-to-all | bytes 4194304 | tf_op jit(solution)/shard_map/all_to_all | solution.py:435
  274.2 21.7 %normal.3 = bf16[32,264,128]{2,1,0:T(8,128)(2,1)S(1)} custom-call(bf16[32,256,128]{2,1,0:T(8,128)(2,1)S(1)} %all_to_all.28.spec_ref, f32[32,512]{1,0:T(8,128)S(1)} %get-tuple-element.26.gains_ref, f32[64]{0:T(128)S(1)} %copy-done.1, f32[8,128]{1,0:T(8,128)S(1)} %get-tuple-element.21.along_ref, bf16[64,2,512,256]{3,2,1,0:T(8,128)(2,1)} %w_hbm.5), custom_call_target="tpu_custom_call" | custom-call | tf_op jit(solution)/shard_map/normal/pallas_call | solution.py:468
  295.9 53.7 %all_to_all.29.back_ref = bf16[32,264,128]{2,1,0:T(8,128)(2,1)S(1)} all-to-all(bf16[32,264,128]{2,1,0:T(8,128)(2,1)S(1)} %normal.3), channel_id=1, replica_groups=mesh['row'=4,'col'=8] {'row','col'}, dimensions={0} | all-to-all | bytes 4325376 | tf_op jit(solution)/shard_map/all_to_all | solution.py:435
  349.7 5.9 %last_taps.1 = (f32[256,1024]{1,0:T(8,128)}, f32[256,1024]{1,0:T(8,128)}) custom-call(bf16[32,264,128]{2,1,0:T(8,128)(2,1)S(1)} %all_to_all.29.back_ref, f32[256,1024]{1,0:T(8,128)S(1)} %get-tuple-element.19.rhs_ref, f32[256,1024]{1,0:T(8,128)S(1)} %get-tuple-element.22.residual_ref, f32[8,128]{1,0:T(8,128)S(1)} %get-tuple-element.23.step_ref, ...), custom_call_target="tpu_custom_call" | custom-call | tf_op jit(solution)/shard_map/last_taps/pallas_call | solution.py:469
  (3 shorter events, 0.0 us)
Async XLA Ops:
  18.1 66.6 %copy-start = (bf16[4096,1024]{1,0:T(8,128)(2,1)}, bf16[4096,1024]{1,0:T(8,128)(2,1)S(1)}, u32[]{:S(2)}) copy-start(bf16[4096,1024]{1,0:T(8,128)(2,1)S(1)} %get-tuple-element.16.low_ref) | copy-start | bytes 25165828
  84.7 52.2 %copy-start.1 = (f32[64]{0:T(128)S(1)}, f32[64]{0:T(128)}, u32[]{:S(2)}) copy-start(f32[64]{0:T(128)} %reg_ref.3) | copy-start | bytes 772
  136.9 75.7 %slice-start = ((s8[8388608]{0:T(1024)(128)(4,1)}), s8[4194304]{0:T(1024)(128)(4,1)S(1)}, s32[]{:S(2)}) async-start(s8[8388608]{0:T(1024)(128)(4,1)} %bitcast.4), calls=%async_computation.5 | async-start | bytes 8388608
  136.9 75.7 %slice-start.1 = ((s8[8388608]{0:T(1024)(128)(4,1)}), s8[4194304]{0:T(1024)(128)(4,1)S(1)}, s32[]{:S(2)}) async-start(s8[8388608]{0:T(1024)(128)(4,1)} %bitcast.4), calls=%async_computation.6 | async-start | bytes 8388608

commit v4 on v3

--- a/solution.py
+++ b/solution.py
@@ -314,7 +314,7 @@
     store_sums(out_ref, along_ref[...], jnp.sum(bend))
 
 
-PIECES = 4
+PIECES = 2
 
 
 def taps_of(back_ref, high_ref, low_ref, count):

time: 356 us -> 355 us (level)
  no operation moved by 1% of the time
where the time goes in v4:
time: 355 us
  blocking collectives  269 us (76%)
  Pallas kernels  83.5 us (24%)
    all_to_all x5, blocking collectives, exchange(): lax.all_to_all(payload, AXES, split_axis=0, concat_axis=0, tiled=True)  269 us
    pallas_call x2, Pallas kernels, kernel_body(): back = normal(exchange(spec), gains, reg_weight, along, transfer)  43.8 us
    pallas_call x1, Pallas kernels, kernel_body(): call(rhs_kernel, 'rhs_back', [vmem()] * 4 + [hbm(), hbm()], [block, table...  15.8 us
    pallas_call x1, Pallas kernels, kernel_body(): call(middle_kernel, 'middle_taps', [vmem()] * 5, [taps, block, tile, tile])  9.08 us
    pallas_call x1, Pallas kernels, kernel_body(): call(first_kernel, 'first_taps', [vmem()] * 3, [taps, block, tile])  8.93 us

profile of v4, /device:TPU:0, one launch (start us, length us, event | category | flops | bytes accessed | tf_op | source)
XLA Modules:
  0.0 354.5 jit_solution(1740921544635715625)
XLA Ops:
  1.3 0.9 broadcast_select_fusion
  2.2 15.8 %rhs_back.1 = (bf16[32,256,128]{2,1,0:T(8,128)(2,1)S(1)}, bf16[4096,1024]{1,0:T(8,128)(2,1)S(1)}, bf16[4096,1024]{1,0:T(8,128)(2,1)S(1)}) custom-call(f32[32,512]{1,0:T(8,128)S(1)} %convert_element_type.3.bright_ref, f32[32,512]{1,0:T(8,128)S(1)} %get-tuple-element.26.gains_ref, f32[8,128]{1,0:T(8,128)S(1)} %broadcast_in_dim.20.momentum_ref, ...), custom_call_target="tpu_custom_call" | custom-call | tf_op jit(solution)/shard_map/rhs_back/pallas_call | solution.py:455
  18.1 0.0 copy-start
  18.1 57.2 %all_to_all.25.back_ref = bf16[32,256,128]{2,1,0:T(8,128)(2,1)S(1)} all-to-all(bf16[32,256,128]{2,1,0:T(8,128)(2,1)S(1)} %get-tuple-element.14), channel_id=1, replica_groups=mesh['row'=4,'col'=8] {'row','col'}, dimensions={0} | all-to-all | bytes 4194304 | tf_op jit(solution)/shard_map/all_to_all | solution.py:435
  75.3 8.9 %first_taps.1 = (f32[256,1024]{1,0:T(8,128)S(1)}, bf16[32,256,128]{2,1,0:T(8,128)(2,1)S(1)}, f32[8,128]{1,0:T(8,128)S(1)}) custom-call(bf16[32,256,128]{2,1,0:T(8,128)(2,1)S(1)} %all_to_all.25.back_ref, bf16[4096,1024]{1,0:T(8,128)(2,1)S(1)} %get-tuple-element.15.high_ref, bf16[4096,1024]{1,0:T(8,128)(2,1)S(1)} %get-tuple-element.16.low_ref), custom_call_target="tpu_custom_call" | custom-call | tf_op jit(solution)/shard_map/first_taps/pallas_call | solution.py:461
  84.2 0.0 copy-done
  84.2 0.0 copy-start.1
  84.2 52.1 %all_to_all.26.spec_ref = bf16[32,256,128]{2,1,0:T(8,128)(2,1)S(1)} all-to-all(bf16[32,256,128]{2,1,0:T(8,128)(2,1)S(1)} %get-tuple-element.17), channel_id=1, replica_groups=mesh['row'=4,'col'=8] {'row','col'}, dimensions={0} | all-to-all | bytes 4194304 | tf_op jit(solution)/shard_map/all_to_all | solution.py:435
  136.3 0.0 slice-start
  136.3 0.0 copy-done.1
  136.3 0.0 slice-start.1
  136.3 22.0 %normal.2 = bf16[32,264,128]{2,1,0:T(8,128)(2,1)S(1)} custom-call(bf16[32,256,128]{2,1,0:T(8,128)(2,1)S(1)} %all_to_all.26.spec_ref, f32[32,512]{1,0:T(8,128)S(1)} %get-tuple-element.26.gains_ref, f32[64]{0:T(128)S(1)} %copy-done.1, f32[8,128]{1,0:T(8,128)S(1)} %get-tuple-element.18.along_ref, bf16[64,2,512,256]{3,2,1,0:T(8,128)(2,1)} %w_hbm.5), custom_call_target="tpu_custom_call" | custom-call | tf_op jit(solution)/shard_map/normal/pallas_call | solution.py:464
  158.4 53.7 %all_to_all.27.back_ref = bf16[32,264,128]{2,1,0:T(8,128)(2,1)S(1)} all-to-all(bf16[32,264,128]{2,1,0:T(8,128)(2,1)S(1)} %normal.2), channel_id=1, replica_groups=mesh['row'=4,'col'=8] {'row','col'}, dimensions={0} | all-to-all | bytes 4325376 | tf_op jit(solution)/shard_map/all_to_all | solution.py:435
  212.1 0.0 slice-done
  212.1 0.0 slice-done.1
  212.1 9.1 %middle_taps.1 = (f32[256,1024]{1,0:T(8,128)S(1)}, bf16[32,256,128]{2,1,0:T(8,128)(2,1)S(1)}, f32[8,128]{1,0:T(8,128)S(1)}, f32[8,128]{1,0:T(8,128)S(1)}) custom-call(bf16[32,264,128]{2,1,0:T(8,128)(2,1)S(1)} %all_to_all.27.back_ref, f32[256,1024]{1,0:T(8,128)S(1)} %get-tuple-element.19.rhs_ref, f32[8,128]{1,0:T(8,128)S(1)} %broadcast_in_dim.20.momentum_ref, ...), custom_call_target="tpu_custom_call" | custom-call | tf_op jit(solution)/shard_map/middle_taps/pallas_call | solution.py:465
  221.2 52.0 %all_to_all.28.spec_ref = bf16[32,256,128]{2,1,0:T(8,128)(2,1)S(1)} all-to-all(bf16[32,256,128]{2,1,0:T(8,128)(2,1)S(1)} %get-tuple-element.20), channel_id=1, replica_groups=mesh['row'=4,'col'=8] {'row','col'}, dimensions={0} | all-to-all | bytes 4194304 | tf_op jit(solution)/shard_map/all_to_all | solution.py:435
  273.1 21.8 %normal.3 = bf16[32,264,128]{2,1,0:T(8,128)(2,1)S(1)} custom-call(bf16[32,256,128]{2,1,0:T(8,128)(2,1)S(1)} %all_to_all.28.spec_ref, f32[32,512]{1,0:T(8,128)S(1)} %get-tuple-element.26.gains_ref, f32[64]{0:T(128)S(1)} %copy-done.1, f32[8,128]{1,0:T(8,128)S(1)} %get-tuple-element.21.along_ref, bf16[64,2,512,256]{3,2,1,0:T(8,128)(2,1)} %w_hbm.5), custom_call_target="tpu_custom_call" | custom-call | tf_op jit(solution)/shard_map/normal/pallas_call | solution.py:468
  294.9 53.7 %all_to_all.29.back_ref = bf16[32,264,128]{2,1,0:T(8,128)(2,1)S(1)} all-to-all(bf16[32,264,128]{2,1,0:T(8,128)(2,1)S(1)} %normal.3), channel_id=1, replica_groups=mesh['row'=4,'col'=8] {'row','col'}, dimensions={0} | all-to-all | bytes 4325376 | tf_op jit(solution)/shard_map/all_to_all | solution.py:435
  348.6 5.9 %last_taps.1 = (f32[256,1024]{1,0:T(8,128)}, f32[256,1024]{1,0:T(8,128)}) custom-call(bf16[32,264,128]{2,1,0:T(8,128)(2,1)S(1)} %all_to_all.29.back_ref, f32[256,1024]{1,0:T(8,128)S(1)} %get-tuple-element.19.rhs_ref, f32[256,1024]{1,0:T(8,128)S(1)} %get-tuple-element.22.residual_ref, f32[8,128]{1,0:T(8,128)S(1)} %get-tuple-element.23.step_ref, ...), custom_call_target="tpu_custom_call" | custom-call | tf_op jit(solution)/shard_map/last_taps/pallas_call | solution.py:469
  (3 shorter events, 0.0 us)
Async XLA Ops:
  18.1 66.1 %copy-start = (bf16[4096,1024]{1,0:T(8,128)(2,1)}, bf16[4096,1024]{1,0:T(8,128)(2,1)S(1)}, u32[]{:S(2)}) copy-start(bf16[4096,1024]{1,0:T(8,128)(2,1)S(1)} %get-tuple-element.16.low_ref) | copy-start | bytes 25165828
  84.2 52.2 %copy-start.1 = (f32[64]{0:T(128)S(1)}, f32[64]{0:T(128)}, u32[]{:S(2)}) copy-start(f32[64]{0:T(128)} %reg_ref.3) | copy-start | bytes 772
  136.3 75.7 %slice-start = ((s8[8388608]{0:T(1024)(128)(4,1)}), s8[4194304]{0:T(1024)(128)(4,1)S(1)}, s32[]{:S(2)}) async-start(s8[8388608]{0:T(1024)(128)(4,1)} %bitcast.4), calls=%async_computation.5 | async-start | bytes 8388608
  136.3 75.7 %slice-start.1 = ((s8[8388608]{0:T(1024)(128)(4,1)}), s8[4194304]{0:T(1024)(128)(4,1)S(1)}, s32[]{:S(2)}) async-start(s8[8388608]{0:T(1024)(128)(4,1)} %bitcast.4), calls=%async_computation.6 | async-start | bytes 8388608
